TPU v7x, 256 devices: a whole 4x4x8 slice. The times are simulated.
256 devices in a mesh: row: 16 (over x, z_lo), col: 16 (over y, z_hi, core).
Axes of the slice: x: 4, y: 4, z: 8 (z_hi: 2, z_lo: 4; z = z_hi * 4 + z_lo), core: 2. Of those that a mesh axis runs over, the one named last changes fastest.
Arguments:
- potential: float32 [32, 64, 512], P('row', 'col'), may hold values from -6 to 6
- basis: bfloat16 [32, 64, 384, 512], P('row', 'col'), may hold values from -6 to 6
- hamiltonian: bfloat16 [6144, 6144], P('row', 'col'), may hold values from -0.078125 to 0.078125
- density: bfloat16 [2, 6144, 6144], P(None, 'row', 'col'), may hold values from -6 to 6
- hmask: int32 [48, 48], replicated, may hold values from 0 to 1, as said below
- pmask: int32 [48, 48], replicated, may hold values from 0 to 1, as said below
Outputs:
- propagated: bfloat16 [2, 6144, 6144], P(None, 'row', 'col')
Inputs may be any that keep to these rules, and one draw needn't show every extreme that they name: hmask[I, I] is always 1; every other block is 1 with probability 1/2, independently. pmask follows the same law as hmask, drawn independently.
All inputs are finite; a program needn't handle non-finite values.
Results may differ from a plain program's by a relative error of at most 0.0062.
Values may be sent and summed in bfloat16 or wider, within the bound.
A program may use at most 64 MiB of HBM per device.

v0:
```python
import jax
import jax.numpy as jnp
from jax import lax
from jax.sharding import PartitionSpec as P

BLK = 128


KAPPA = 0.4
TIME_STEP = 0.5


def extended_2(block, sides, width):
    for axis, dim in sides:
        count = lax.axis_size(axis)
        forward = [(i, i + 1) for i in range(count - 1)]
        backward = [(target, source) for source, target in forward]
        low = lax.ppermute(
            lax.slice_in_dim(block, block.shape[dim] - width, None, axis=dim), axis, forward
        )
        high = lax.ppermute(lax.slice_in_dim(block, 0, width, axis=dim), axis, backward)
        block = jnp.concatenate([low, block, high], axis=dim)
    return block


def shards(potential, basis, hamiltonian, density, hmask, pmask):
    width_x, width_y, depth_z = potential.shape
    extended = extended_2(potential, (("row", 0), ("col", 1)), 1)
    padded = jnp.pad(extended, ((0, 0), (0, 0), (1, 1)))
    beside = padded[2:, 1:-1, 1:-1] + padded[:-2, 1:-1, 1:-1]
    beside = beside + padded[1:-1, 2:, 1:-1] + padded[1:-1, :-2, 1:-1]
    beside = beside + padded[1:-1, 1:-1, 2:] + padded[1:-1, 1:-1, :-2]
    effective = potential + KAPPA * (beside - 6.0 * potential)
    blocks_here = basis.shape[2] // BLK
    weighted = (basis * effective[:, :, None, :]).astype(jnp.bfloat16)
    partial_blocks = jnp.einsum(
        "xykaz,xykbz->kab",
        weighted.reshape(width_x, width_y, blocks_here, BLK, depth_z),
        basis.reshape(width_x, width_y, blocks_here, BLK, depth_z),
        preferred_element_type=jnp.float32,
    )
    summed = lax.psum(partial_blocks, "col")
    factor = float(BLK * width_x * width_y * depth_z * lax.axis_size("col")) ** (-0.5)
    potential_blocks = (summed * factor).astype(jnp.bfloat16)
    block_total = hmask.shape[0]
    blocks_wide = block_total // lax.axis_size("col")
    row_start = lax.axis_index("row") * blocks_here
    col_start = lax.axis_index("col") * blocks_wide
    hpattern = lax.dynamic_slice(hmask, (row_start, col_start), (blocks_here, blocks_wide))
    ppattern = lax.dynamic_slice(pmask, (row_start, col_start), (blocks_here, blocks_wide))
    masked_h = (
        hamiltonian.reshape(blocks_here, BLK, blocks_wide, BLK)
        * hpattern[:, None, :, None].astype(jnp.bfloat16)
    ).reshape(blocks_here * BLK, blocks_wide * BLK)
    masked_p = (
        density.reshape(2, blocks_here, BLK, blocks_wide, BLK)
        * ppattern[None, :, None, :, None].astype(jnp.bfloat16)
    ).reshape(2, blocks_here * BLK, blocks_wide * BLK)

    def diagonal_term(operand):
        local = jnp.einsum(
            "kab,skbc->skac",
            potential_blocks,
            operand.reshape(2, blocks_here, BLK, operand.shape[2]),
            preferred_element_type=jnp.float32,
        )
        return local.reshape(2, blocks_here * BLK, operand.shape[2])

    def apply(operand):
        column_whole = lax.all_gather(operand, "row", axis=1, tiled=True)
        remote = jnp.einsum(
            "rk,skc->src",
            lax.all_gather(masked_h, "col", axis=1, tiled=True),
            column_whole,
            preferred_element_type=jnp.float32,
        )
        return remote + diagonal_term(operand)

    first = apply(masked_p)
    first_rounded = first.astype(jnp.bfloat16)
    second = apply(first_rounded)
    base = masked_p.astype(jnp.float32)
    half_square = 0.5 * TIME_STEP * TIME_STEP
    real_part = base[0] + TIME_STEP * first[1] - half_square * second[0]
    imag_part = base[1] - TIME_STEP * first[0] - half_square * second[1]
    stacked = jnp.stack([real_part, imag_part]).reshape(2, blocks_here, BLK, blocks_wide, BLK)
    stacked = stacked * ppattern[None, :, None, :, None].astype(jnp.float32)
    return stacked.reshape(2, blocks_here * BLK, blocks_wide * BLK).astype(jnp.bfloat16)


def solution(mesh):
    in_specs = (
        P("row", "col", None),
        P("row", "col", None, None),
        P("row", "col"),
        P(None, "row", "col"),
        P(),
        P(),
    )
    out_specs = P(None, "row", "col")
    return jax.shard_map(shards, mesh=mesh, in_specs=in_specs, out_specs=out_specs, check_vma=False)
```

profile of v0, /device:TPU:1, one launch (start us, length us, event | category | flops | bytes accessed | tf_op | source)
XLA Modules:
  0.0 729.8 jit_solution(5748484860902074060)
XLA Ops:
  6.5 0.7 fusion.37
  7.3 4.3 collective-permute-start.1
  11.6 1.3 collective-permute-start
  12.9 0.7 constant_dynamic-update-slice_fusion.1
  13.7 2.5 collective-permute-done
  16.2 3.8 collective-permute-start.2
  20.1 7.8 %collective-permute-start.3 = (f32[4,1,512]{2,1,0:T(1,128)S(1)}, f32[4,1,512]{2,1,0:T(1,128)S(1)}, u32[]{:S(2)}, u32[]{:S(2)}) collective-permute-start(f32[4,1,512]{2,1,0:T(1,128)S(1)} %get-tuple-element.9), channel_id=1, source_target_pairs={{0,1},{1,2},{2,3},{3,4},{4,5},{5,6},{6,7},{7,8},{8,9},{9,10},{10,1... | collective-permute-start | bytes 24584 | tf_op jit(solution)/shard_map/ppermute | solution.py:18
  27.9 0.8 dynamic-slice_convert_fusion.1
  28.8 0.9 fusion.29
  29.7 2.7 multiply_convert_fusion
  32.6 1.7 convolution_bitcast_fusion.2
  34.5 0.8 bitcast_multiply_fusion
  35.6 0.9 fusion.35
  36.7 175.1 %all-reduce.3.cloned.1.call-done = f32[3,128,128]{2,1,0:T(8,128)} async-done(((f32[3,128,128]{2,1,0:T(8,128)}), f32[3,128,128]{2,1,0:T(8,128)}) %all-reduce.3.cloned.1.call-update) | async-done | bytes 196624 | tf_op jit(solution)/shard_map/psum | solution.py:42
  211.8 1.2 convolution_bitcast_fusion.1
  213.2 82.5 %all-gather.6.cloned.1.call-done = bf16[384,6144]{1,0:T(8,128)(2,1)} async-done(((bf16[384,384]{1,0:T(8,128)(2,1)}), bf16[384,6144]{1,0:T(8,128)(2,1)}) %all-gather.6.cloned.1.call-update) | async-done | bytes 4718608 | tf_op jit(solution)/shard_map/all_gather | solution.py:73
  295.7 203.1 %all-gather.4.cloned.1.call-done = bf16[2,6144,384]{2,1,0:T(8,128)(2,1)} async-done(((bf16[2,384,384]{2,1,0:T(8,128)(2,1)}), bf16[2,6144,384]{2,1,0:T(8,128)(2,1)}) %all-gather.4.cloned.1.call-update) | async-done | bytes 9437200 | tf_op jit(solution)/shard_map/all_gather | solution.py:70
  498.8 10.2 %fusion.38 = (bf16[2,384,384]{2,1,0:T(8,128)(2,1)}, f32[2,384,384]{2,1,0:T(8,128)}) fusion(f32[2,384,384]{2,1,0:T(8,128)S(1)} %bitcast.74, bf16[2,6144,384]{2,1,0:T(8,128)(2,1)} %all-gather.4.cloned.1.call-done, bf16[384,6144]{1,0:T(8,128)(2,1)} %all-gather.6.cloned.1.call-done), kind=kOutput, calls=%fused_computation.61 | convolution fusion | flops 3624468480 | bytes 17104896 | tf_op jit(solution)/shard_map/rk,skc->src/dot_general | solution.py:71
  509.2 0.8 copy-done.1
  510.0 0.3 convolution_bitcast_fusion
  510.4 203.2 %all-gather.8.cloned.1.call-done = bf16[2,6144,384]{2,1,0:T(8,128)(2,1)} async-done(((bf16[2,384,384]{2,1,0:T(8,128)(2,1)}), bf16[2,6144,384]{2,1,0:T(8,128)(2,1)}) %all-gather.8.cloned.1.call-update) | async-done | bytes 9437200 | tf_op jit(solution)/shard_map/all_gather | solution.py:70
  713.6 8.5 %fusion.13 = f32[2,384,384]{2,1,0:T(8,128)S(1)} fusion(f32[2,384,384]{2,1,0:T(8,128)S(1)} %bitcast.75, bf16[2,6144,384]{2,1,0:T(8,128)(2,1)} %all-gather.8.cloned.1.call-done, bf16[384,6144]{1,0:T(8,128)(2,1)} %all-gather.6.cloned.1.call-done), kind=kOutput, calls=%fused_computation.10 | convolution fusion | flops 3624173568 | bytes 16515072 | tf_op jit(solution)/shard_map/rk,skc->src/dot_general | solution.py:71
  722.1 0.3 fusion.19
  722.4 0.9 fusion.16
  (35 shorter events, 1.3 us)
Async XLA Ops:
  6.5 205.3 %all-reduce.3.cloned.1.call-start = ((), (), s32[]{:S(2)}) async-start(), calls=%async_computation.2 | async-start | bytes 393216 | tf_op jit(solution)/shard_map/psum | solution.py:42
  7.3 5.7 collective-permute-start.1
  11.6 4.6 collective-permute-start
  16.2 12.5 %collective-permute-start.2 = (f32[4,1,512]{2,1,0:T(1,128)S(1)}, f32[4,1,512]{2,1,0:T(1,128)S(1)}, u32[]{:S(2)}, u32[]{:S(2)}) collective-permute-start(f32[4,1,512]{2,1,0:T(1,128)S(1)} %get-tuple-element.10), channel_id=1, source_target_pairs={{1,0},{2,1},{3,2},{4,3},{5,4},{6,5},{7,6},{8,7},{9,8},{10,9},{11,1... | collective-permute-start | bytes 24584 | tf_op jit(solution)/shard_map/ppermute | solution.py:21
  20.1 8.6 %collective-permute-start.3 = (f32[4,1,512]{2,1,0:T(1,128)S(1)}, f32[4,1,512]{2,1,0:T(1,128)S(1)}, u32[]{:S(2)}, u32[]{:S(2)}) collective-permute-start(f32[4,1,512]{2,1,0:T(1,128)S(1)} %get-tuple-element.9), channel_id=1, source_target_pairs={{0,1},{1,2},{2,3},{3,4},{4,5},{5,6},{6,7},{7,8},{8,9},{9,10},{10,1... | collective-permute-start | bytes 24584 | tf_op jit(solution)/shard_map/ppermute | solution.py:18
  29.7 2.8 copy-start
  32.6 1.9 copy-start.5
  32.6 3.0 copy-start.2
  34.2 261.5 %all-gather.6.cloned.1.call-start = ((), (), s32[]{:S(2)}) async-start(), calls=%async_computation.1 | async-start | bytes 5013504 | tf_op jit(solution)/shard_map/all_gather | solution.py:73
  35.3 463.5 %all-gather.4.cloned.1.call-start = ((), (), s32[]{:S(2)}) async-start(), calls=%async_computation | async-start | bytes 10027008 | tf_op jit(solution)/shard_map/all_gather | solution.py:70
  36.6 677.0 %all-gather.8.cloned.1.call-start = ((), (), s32[]{:S(2)}) async-start(), calls=%async_computation.3 | async-start | bytes 10027008 | tf_op jit(solution)/shard_map/all_gather | solution.py:70
  498.8 10.4 %copy-start.4 = (f32[3,128,128]{2,1,0:T(8,128)S(1)}, f32[3,128,128]{2,1,0:T(8,128)}, u32[]{:S(2)}) copy-start(f32[3,128,128]{2,1,0:T(8,128)} %all-reduce.3.cloned.1.call-done) | copy-start | bytes 589828
  508.9 1.1 copy-start.1
  713.6 8.5 %copy-start.3 = (f32[2,384,384]{2,1,0:T(8,128)S(1)}, f32[2,384,384]{2,1,0:T(8,128)}, u32[]{:S(2)}) copy-start(f32[2,384,384]{2,1,0:T(8,128)} %get-tuple-element.16) | copy-start | bytes 3538948
Sparse Core Ops, SparseCore 0:
  34.4 177.4 all-reduce.2
  214.4 81.2 all-gather.5
  297.5 201.2 all-gather.3
  509.1 204.4 all-gather.7
where the time goes:
time: 730 us
  waiting for transfers between devices  667 us (91%)
  matrix products  21.9 us (3%)
  starting transfers between devices  17.4 us (2%)
  between operations  13.3 us (2%)
  other arithmetic  7.46 us (1%)
    all_gather x2, waiting for transfers between devices, apply(): column_whole = lax.all_gather(operand, 'row', axis=1, tiled=True)  406 us
    psum x1, waiting for transfers between devices, shards(): summed = lax.psum(partial_blocks, 'col')  175 us
    all_gather x1, waiting for transfers between devices, apply(): lax.all_gather(masked_h, 'col', axis=1, tiled=True)  82.5 us
    dot_general x2, matrix products, apply(): jnp.einsum('rk,skc->src', lax.all_gather(masked_h, 'col', axis=1, tiled=T...  18.7 us
  transfers between devices with their start and end apart: 8, of which 5 were waited for; matrix products, arithmetic and copies ran while one was open for 1% of the time, Pallas kernels for 0%

commit v1 on v0

v1 whole, which is shorter than its diff:
```python
import functools
import heapq

import jax
import jax.numpy as jnp
from jax import lax
from jax.experimental import pallas as pl
from jax.experimental.pallas import tpu as pltpu
from jax.sharding import PartitionSpec as P

BLK = 128
KAPPA = 0.4
TIME_STEP = 0.5
MESH = pl.DeviceIdType.MESH

STEPS = 3
Y_FIRST = (16, 16, 32)
ROWS = 64
WIDE = 384


def plus_hops(s):
    return 4 if s % 2 == 0 else 3


def antipode_plus(dz):
    return dz % 2 == 0


def messages():
    out = {}
    for s in range(STEPS):
        a_kb, b_kb = Y_FIRST[s] * 1.5, (ROWS - Y_FIRST[s]) * 1.5
        out["Hm", s] = ("m", 48, [], ("H", s))
        up, down = plus_hops(s), 7 - plus_hops(s)
        for t in range(1, up + 1):
            out["bz+", s, t] = ("z+", b_kb, [("b", s, 0, 1 - t)], ("b", s, 0, -t))
        for t in range(1, down + 1):
            out["bz-", s, t] = ("z-", b_kb, [("b", s, 0, t - 1)], ("b", s, 0, t))
        for dz in range(-up, down + 1):
            out["by+", s, dz] = ("y+", b_kb, [("b", s, 0, dz)], ("b", s, -1, dz))
            out["by-", s, dz] = ("y-", b_kb, [("b", s, 0, dz)], ("b", s, 1, dz))
            if antipode_plus(dz):
                out["by2", s, dz] = ("y+", b_kb, [("b", s, -1, dz)], ("b", s, 2, dz))
            else:
                out["by2", s, dz] = ("y-", b_kb, [("b", s, 1, dz)], ("b", s, 2, dz))
        out["ay+", s] = ("y+", a_kb, [("a", s, 0)], ("a", s, -1))
        out["ay-", s] = ("y-", a_kb, [("a", s, 0)], ("a", s, 1))
        if s % 2 == 0:
            out["ay2", s] = ("y+", a_kb, [("a", s, -1)], ("a", s, 2))
        else:
            out["ay2", s] = ("y-", a_kb, [("a", s, 1)], ("a", s, 2))
        whole = [("a", s, 0), ("a", s, -1), ("a", s, 1), ("a", s, 2)]
        for t in range(1, up + 1):
            needs = whole if t == 1 else [("A4", s, 1 - t)]
            out["az+", s, t] = ("z+", 4 * a_kb, needs, ("A4", s, -t))
        for t in range(1, down + 1):
            needs = whole if t == 1 else [("A4", s, t - 1)]
            out["az-", s, t] = ("z-", 4 * a_kb, needs, ("A4", s, t))
    for rb in range(4):
        out["Px+", rb] = ("x+", 144, [("P", 0, rb)], ("P", -1, rb))
        out["Px-", rb] = ("x-", 144, [("P", 0, rb)], ("P", 1, rb))
        if rb < 2:
            out["Px2", rb] = ("x+", 144, [("P", -1, rb)], ("P", 2, rb))
        else:
            out["Px2", rb] = ("x-", 144, [("P", 1, rb)], ("P", 2, rb))
        for dx in (0, -1, 1, 2):
            out["Pm", dx, rb] = ("m", 144, [("P", dx, rb)], ("Pm", dx, rb))
    for s in range(STEPS):
        out["Fx+", s] = ("x+", 192, [("F", 0, s)], ("F", -1, s))
        out["Fx-", s] = ("x-", 192, [("F", 0, s)], ("F", 1, s))
        out["F2+", s] = ("x+", 96, [("F", -1, s)], ("F2", 0, s))
        out["F2-", s] = ("x-", 96, [("F", 1, s)], ("F2", 1, s))
        for dx in (0, -1, 1):
            out["Fm", dx, s] = ("m", 192, [("F", dx, s)], ("Fm", dx, s))
        for e in (0, 1):
            out["Fm2", e, s] = ("m", 96, [("F2", e, s)], ("Fm2", e, s))
    out["Dm",] = ("m", 96, [], ("Dm",))
    for j in range(1, 8):
        out["Dr", j] = ("z+" if j % 2 else "y+", 12, [("Dc",)], ("Dr", j))
    for j in range(1, 4):
        out["Dy", j] = ("y-", 12, [("Df",)], ("Dy", j))
    for j in range(1, 8):
        out["Dz", j] = ("z-", 48, [("Df",)] + [("Dy", i) for i in (1, 2, 3)], ("Dz", j))
    return out


def tasks():
    out = {}
    for s in range(STEPS):
        out["Hready", s] = (0.05, [("H", s)], [("b", s, 0, 0), ("a", s, 0)])
    every_p = [("P", dx, rb) for dx in (0, -1, 1, 2) for rb in range(4)]
    every_p += [("Pm", dx, rb) for dx in (0, -1, 1, 2) for rb in range(4)]
    every_d = [("Dy", i) for i in (1, 2, 3)] + [("Dz", i) for i in range(1, 8)] + [("Df",)]
    for s in range(STEPS):
        up, down = plus_hops(s), 7 - plus_hops(s)
        near = [("b", s, dy, dz) for dy in (0, -1, 1) for dz in range(-up, down + 1)]
        near += [("A4", s, dz) for dz in range(-up, down + 1) if dz] + [("a", s, 2)]
        far = [("b", s, 2, dz) for dz in range(-up, down + 1)]
        out["C1", s] = (3.2, near + far + every_p, [("C1", s)])
        out["Ff", s] = (0.5, [("C1", s)] + every_d, [("F", 0, s)])
    out["Dc",] = (0.2, [("Dm",)], [("Dc",)])
    out["Df",] = (0.2, [("Dc",)] + [("Dr", j) for j in range(1, 8)], [("Df",)])
    all_a = [("C1", s) for s in range(STEPS)]
    for s in range(STEPS):
        out["S", s, 0] = (0.9, all_a + [("F", 0, s), ("Fm", 0, s)], [("S", s, 0)])
        out["S", s, -1] = (0.8, all_a + [("F", -1, s), ("Fm", -1, s)], [("S", s, -1)])
        out["S", s, 1] = (0.8, all_a + [("F", 1, s), ("Fm", 1, s)], [("S", s, 1)])
        far = [("F2", e, s) for e in (0, 1)] + [("Fm2", e, s) for e in (0, 1)]
        out["S", s, 2] = (0.8, all_a + far, [("S", s, 2)])
    return out


RATE = {"m": 200.0}
LINK_RATE = 42.0
BACKLOG = 4.0


def rank_of(name):
    kind = name[0]
    if kind in ("Hm", "Dm", "Dr", "Dy", "Dz"):
        return (-1, 0)
    if kind[0] in "PF":
        return (0, 0)
    return (name[1], 0 if kind in ("bz+", "bz-", "ay+", "ay-", "ay2") else 1)


def schedule():
    every, work = messages(), tasks()
    given_by = {m[3]: n for n, m in every.items()}
    have, sent, done = set(), set(), set()
    free = {}
    arrivals = []
    order = []
    now = 0.0
    free["z+"] = free["z-"] = 2 * 144 / LINK_RATE / 1.0
    for rb in range(4):
        heapq.heappush(arrivals, (16.0 + rb, 0, ("P0", rb)))
    count = 0

    def issue():
        nonlocal count
        ready = [n for n, m in every.items() if n not in sent and all(d in have for d in m[2])]
        ready.sort(key=rank_of)
        for name in ready:
            link, size, _, _ = every[name]
            start = max(now, free.get(link, 0.0))
            if start - now > BACKLOG and link != "m":
                continue
            end = start + size / RATE.get(link, LINK_RATE)
            free[link] = end
            sent.add(name)
            count += 1
            heapq.heappush(arrivals, (end + (1.0 if link == "m" else 1.8), count, name))
            order.append(("send", name))

    while len(done) < len(work) or arrivals:
        issue()
        if arrivals and arrivals[0][0] <= now:
            _, _, name = heapq.heappop(arrivals)
            order.append(("wait", name))
            have.add(("P", 0, name[1]) if name[0] == "P0" else every[name][3])
            continue
        ready = [n for n, w in work.items() if n not in done and all(d in have for d in w[1])]
        if ready:
            name = ready[0]
            now += work[name][0]
            done.add(name)
            have.update(work[name][2])
            order.append(("work", name))
            continue
        later = [arrivals[0][0]] if arrivals else []
        waiting = [n for n, m in every.items() if n not in sent and all(d in have for d in m[2])]
        later += [free[every[n][0]] - BACKLOG + 0.01 for n in waiting]
        now = max(now + 0.01, min(later))
    return order, now


def core_kernel(order, h_ref, p_ref, part_ref, out_ref, a_buf, b_buf, f_buf, o_buf,
                f_acc, s_acc, d_mate, d_chip, d_all, d_got, d_fin,
                send_sem, recv_sem, local_sem, pin_sem, pin_send, ret_sem, ret_send):
    row, col = lax.axis_index("row"), lax.axis_index("col")
    x, zl = row // 4, row % 4
    y, zh, c = col // 4, (col // 2) % 2, col % 2
    z = zh * 4 + zl
    half = c

    def dev(dx=0, dy=0, dz=0, core=None):
        zz = (z + dz) % 8
        core = c if core is None else core
        return (((x + dx) % 4) * 4 + zz % 4, ((y + dy) % 4) * 4 + (zz // 4) * 2 + core)

    def dev_line(q, core):
        return (x * 4 + q, y * 4 + zh * 2 + core)

    barrier = pltpu.get_barrier_semaphore()
    friends = [dev(core=1 - c), dev(dx=1), dev(dx=-1)]
    friends += [dev(dy=j) for j in (1, 2, 3)] + [dev(dz=j) for j in range(1, 8)]
    friends += [dev(dy=j, dz=4) for j in (1, 2, 3)]
    friends += [dev_line((zl + j) % 4, 1 - c) for j in (1, 2, 3)]
    for friend in friends:
        pl.semaphore_signal(barrier, inc=1, device_id=friend, device_id_type=MESH)
    pl.semaphore_wait(barrier, len(friends))

    names = list(messages())
    index = {n: i for i, n in enumerate(names)}

    def block(s, dy, dz, color):
        zz = (z + dz) % 8
        rows = pl.ds(0, Y_FIRST[s]) if color == "a" else pl.ds(Y_FIRST[s], ROWS - Y_FIRST[s])
        return a_buf.at[s, (y + dy) % 4, zz // 4, zz % 4, rows]

    def block4(s, dz):
        zz = (z + dz) % 8
        return a_buf.at[s, :, zz // 4, zz % 4, pl.ds(0, Y_FIRST[s])]

    def lanes(core):
        return pl.ds(pl.multiple_of(core * WIDE, 128), WIDE)

    def b_slot(dx, rb, core):
        return b_buf.at[(x + dx) % 4, rb, :, core]

    def f_slot(dx, s, core, rbs):
        return f_buf.at[(x + dx) % 4, rbs, s, core]

    FULL, LOW, HIGH = pl.ds(0, 4), pl.ds(0, 2), pl.ds(2, 2)

    def ends(name):
        kind = name[0]
        if kind == "Hm":
            s = name[1]
            return (h_ref.at[s, 1 - c], a_buf.at[s, y, zh, zl, :, lanes(c)],
                    a_buf.at[s, y, zh, zl, :, lanes(1 - c)], dev(core=1 - c))
        if kind == "bz+":
            _, s, t = name
            src = block(s, 0, 1 - t, "b")
            return src, src, block(s, 0, -t, "b"), dev(dz=1)
        if kind == "bz-":
            _, s, t = name
            src = block(s, 0, t - 1, "b")
            return src, src, block(s, 0, t, "b"), dev(dz=-1)
        if kind == "by+":
            _, s, dz = name
            src = block(s, 0, dz, "b")
            return src, src, block(s, -1, dz, "b"), dev(dy=1)
        if kind == "by-":
            _, s, dz = name
            src = block(s, 0, dz, "b")
            return src, src, block(s, 1, dz, "b"), dev(dy=-1)
        if kind == "by2":
            _, s, dz = name
            way = 1 if antipode_plus(dz) else -1
            src = block(s, -way, dz, "b")
            return src, src, block(s, 2, dz, "b"), dev(dy=way)
        if kind == "ay+":
            src = block(name[1], 0, 0, "a")
            return src, src, block(name[1], -1, 0, "a"), dev(dy=1)
        if kind == "ay-":
            src = block(name[1], 0, 0, "a")
            return src, src, block(name[1], 1, 0, "a"), dev(dy=-1)
        if kind == "ay2":
            way = 1 if name[1] % 2 == 0 else -1
            src = block(name[1], -way, 0, "a")
            return src, src, block(name[1], 2, 0, "a"), dev(dy=way)
        if kind == "az+":
            _, s, t = name
            src = block4(s, 1 - t)
            return src, src, block4(s, -t), dev(dz=1)
        if kind == "az-":
            _, s, t = name
            src = block4(s, t - 1)
            return src, src, block4(s, t), dev(dz=-1)
        if kind == "Px+":
            src = b_slot(0, name[1], c)
            return src, src, b_slot(-1, name[1], c), dev(dx=1)
        if kind == "Px-":
            src = b_slot(0, name[1], c)
            return src, src, b_slot(1, name[1], c), dev(dx=-1)
        if kind == "Px2":
            way = 1 if name[1] < 2 else -1
            src = b_slot(-way, name[1], c)
            return src, src, b_slot(2, name[1], c), dev(dx=way)
        if kind == "Pm":
            _, dx, rb = name
            src = b_slot(dx, rb, c)
            return src, src, b_slot(dx, rb, 1 - c), dev(core=1 - c)
        if kind == "Fx+":
            src = f_slot(0, name[1], c, FULL)
            return src, src, f_slot(-1, name[1], c, FULL), dev(dx=1)
        if kind == "Fx-":
            src = f_slot(0, name[1], c, FULL)
            return src, src, f_slot(1, name[1], c, FULL), dev(dx=-1)
        if kind == "F2+":
            src = f_slot(-1, name[1], c, LOW)
            return src, src, f_slot(2, name[1], c, LOW), dev(dx=1)
        if kind == "F2-":
            src = f_slot(1, name[1], c, HIGH)
            return src, src, f_slot(2, name[1], c, HIGH), dev(dx=-1)
        if kind == "Fm":
            _, dx, s = name
            src = f_slot(dx, s, c, FULL)
            return src, src, f_slot(dx, s, 1 - c, FULL), dev(core=1 - c)
        if kind == "Fm2":
            _, e, s = name
            rbs = HIGH if e else LOW
            src = f_slot(2, s, c, rbs)
            return src, src, f_slot(2, s, 1 - c, rbs), dev(core=1 - c)
        if kind == "Dm":
            return part_ref.at[:, 1 - c], d_mate, d_mate, dev(core=1 - c)
        if kind == "Dr":
            j = name[1]
            dy, dz = j // 2, 4 * (j % 2)
            to = ((y + dy) % 4) * 2 + (zh + j % 2) % 2
            return d_chip.at[to], d_got.at[j - 1], d_got.at[j - 1], dev(dy=dy, dz=dz)
        if kind == "Dy":
            j = name[1]
            return d_fin, d_all.at[zl, y, zh], d_all.at[zl, (y - j) % 4, zh], dev(dy=j)
        if kind == "Dz":
            j = name[1]
            zz = (z - j) % 8
            src = d_all.at[zl, :, zh]
            return src, src, d_all.at[zz % 4, :, zz // 4], dev(dz=j)
        raise KeyError(name)

    def outgoing(name):
        src, dst, _, target = ends(name)
        i = index[name]
        return pltpu.make_async_remote_copy(
            src_ref=src, dst_ref=dst, send_sem=send_sem.at[i], recv_sem=recv_sem.at[i],
            device_id=target, device_id_type=MESH)

    def incoming(name):
        src, _, land, target = ends(name)
        i = index[name]
        return pltpu.make_async_remote_copy(
            src_ref=land, dst_ref=land, send_sem=send_sem.at[i], recv_sem=recv_sem.at[i],
            device_id=target, device_id_type=MESH)

    own = [pltpu.make_async_copy(h_ref.at[s, c], a_buf.at[s, y, zh, zl, :, lanes(c)],
                                 local_sem.at[s]) for s in range(STEPS)]
    for copy in own:
        copy.start()

    def p_copy(hf, r):
        q = 2 * c + hf
        src = p_ref.at[hf, :, r]
        here = (q == zl) & (r == c)
        dst = b_buf.at[x, zl, :, r]

        def local():
            return pltpu.make_async_copy(src, dst, pin_sem.at[zl])

        def remote():
            return pltpu.make_async_remote_copy(
                src_ref=src, dst_ref=dst, send_sem=pin_send.at[hf, r], recv_sem=pin_sem.at[zl],
                device_id=dev_line(q, r), device_id_type=MESH)

        return here, local, remote

    def start_p():
        for hf in range(2):
            for r in range(2):
                here, local, remote = p_copy(hf, r)

                @pl.when(here)
                def _():
                    local().start()

                @pl.when(jnp.logical_not(here))
                def _():
                    remote().start()

    def chunk_a(s, yy, zz):
        return a_buf[s, yy, zz].reshape(4 * ROWS, 2 * WIDE)

    def first_product(s):
        f_acc[s] = jnp.zeros((4 * ROWS, WIDE), jnp.float32)

        def body(k, carry):
            yy, zz = k // 2, k % 2
            right = b_buf[yy, pl.ds(zz * 2, 2)].reshape(2 * WIDE, WIDE)
            f_acc[s] += jnp.dot(chunk_a(s, yy, zz), right, preferred_element_type=jnp.float32)
            return carry

        lax.fori_loop(0, 8, body, 0)

    def diagonal(rb, s):
        return d_all[rb].reshape(STEPS, ROWS, BLK)[s].astype(jnp.bfloat16)

    def first_finish(s):
        for rb in range(4):
            rows = pl.ds(rb * ROWS, ROWS)
            right = b_buf[x, rb, s].reshape(BLK, WIDE)
            total = f_acc[s, rows] + jnp.dot(diagonal(rb, s), right,
                                             preferred_element_type=jnp.float32)
            f_acc[s, rows] = total
            f_buf[x, rb, s, c] = total.astype(jnp.bfloat16)

    def second_product(s, dx):
        xx = (x + dx) % 4
        tile = slice(s * BLK, (s + 1) * BLK), slice(WIDE + s * BLK, WIDE + (s + 1) * BLK)

        def body(k, carry):
            t, zz = k // 2, k % 2
            left = jnp.concatenate(
                [a_buf[t, xx, zz, :, :, cut].reshape(4 * ROWS, BLK) for cut in tile], axis=1)
            right = jnp.concatenate(
                [f_buf[xx, zz * 2 + e, s].reshape(BLK, WIDE) for e in range(2)], axis=0)
            s_acc[t] += jnp.dot(left, right, preferred_element_type=jnp.float32)
            return carry

        lax.fori_loop(0, 6, body, 0)
        if dx == 0:
            for rb in range(4):
                rows = pl.ds(rb * ROWS, ROWS)
                right = f_buf[x, rb, s].reshape(BLK, WIDE)
                s_acc[s, rows] += jnp.dot(diagonal(rb, s), right,
                                          preferred_element_type=jnp.float32)

    def finish_integrals():
        mine = y * 2 + zh
        total = d_chip[mine]
        for j in range(7):
            total = total + d_got[j]
        factor = float(BLK * 2 * 64 * 512) ** -0.5
        d_fin[...] = total * factor
        d_all[zl, y, zh] = total * factor

    def run(name):
        kind = name[0]
        if kind == "Hready":
            own[name[1]].wait()
        elif kind == "C1":
            first_product(name[1])
        elif kind == "Ff":
            first_finish(name[1])
        elif kind == "S":
            second_product(name[1], name[2])
        elif kind == "Dc":
            d_chip[...] = (part_ref[:, c] + d_mate[...]).reshape(8, 24, BLK)
        elif kind == "Df":
            finish_integrals()

    start_p()
    s_acc[...] = jnp.zeros_like(s_acc)
    for what, name in order:
        if what == "send":
            outgoing(name).start()
        elif what == "wait":
            if name[0] == "P0":
                rb = name[1]
                land = b_buf.at[x, rb, :, c]
                pltpu.make_async_copy(land, land, pin_sem.at[rb]).wait()
            else:
                incoming(name).wait_recv()
        else:
            run(name)

    lane = lax.broadcasted_iota(jnp.int32, (ROWS, BLK), 1)
    quarter = 0.5 * TIME_STEP * TIME_STEP

    def back(rb):
        here = (rb == zl) & (zl // 2 == c)
        src = o_buf.at[rb]
        dst = out_ref.at[zl % 2, :, c]

        def local():
            return pltpu.make_async_copy(src, dst, ret_sem.at[zl % 2, c])

        def remote():
            return pltpu.make_async_remote_copy(
                src_ref=src, dst_ref=dst, send_sem=ret_send.at[rb],
                recv_sem=ret_sem.at[zl % 2, c],
                device_id=dev_line(rb, zl // 2), device_id_type=MESH)

        return here, local, remote

    for rb in range(4):
        rows = pl.ds(rb * ROWS, ROWS)
        for s in range(STEPS):
            base = b_buf[x, rb, s, c].astype(jnp.float32)
            f = f_acc[s, rows]
            mixed = f[:, 2 * BLK:]
            turned = pltpu.roll(mixed, BLK // 2, 1)
            turn = jnp.concatenate(
                [f[:, BLK:2 * BLK], -f[:, :BLK], jnp.where(lane < BLK // 2, turned, -turned)],
                axis=1)
            o_buf[rb, s] = (base + TIME_STEP * turn - quarter * s_acc[s, rows]).astype(jnp.bfloat16)
        here, local, remote = back(rb)

        @pl.when(here)
        def _():
            local().start()

        @pl.when(jnp.logical_not(here))
        def _():
            remote().start()

    for hf in range(2):
        for r in range(2):
            land = out_ref.at[hf, :, r]
            pltpu.make_async_copy(land, land, ret_sem.at[hf, r]).wait()

    for what, name in order:
        if what == "send":
            outgoing(name).wait_send()
    for hf in range(2):
        for r in range(2):
            here, _, remote = p_copy(hf, r)

            @pl.when(jnp.logical_not(here))
            def _():
                remote().wait_send()
    for rb in range(4):
        here, _, remote = back(rb)

        @pl.when(jnp.logical_not(here))
        def _():
            remote().wait_send()


def propagate(h, p, part):
    order, _ = schedule()
    total = len(messages())
    bf, f32 = jnp.bfloat16, jnp.float32
    any_space = pl.BlockSpec(memory_space=pl.ANY)
    vmem = pl.BlockSpec(memory_space=pltpu.VMEM)
    return pl.pallas_call(
        functools.partial(core_kernel, order),
        out_shape=jax.ShapeDtypeStruct((2, STEPS, 2, ROWS, WIDE), bf),
        in_specs=[any_space, any_space, vmem],
        out_specs=any_space,
        scratch_shapes=[
            pltpu.VMEM((STEPS, 4, 2, 4, ROWS, 2 * WIDE), bf),
            pltpu.VMEM((4, 4, STEPS, 2, ROWS, WIDE), bf),
            pltpu.VMEM((4, 4, STEPS, 2, ROWS, WIDE), bf),
            pltpu.VMEM((4, STEPS, ROWS, WIDE), bf),
            pltpu.VMEM((STEPS, 4 * ROWS, WIDE), f32),
            pltpu.VMEM((STEPS, 4 * ROWS, WIDE), f32),
            pltpu.VMEM((STEPS, ROWS, BLK), f32),
            pltpu.VMEM((8, 24, BLK), f32),
            pltpu.VMEM((4, 4, 2, 24, BLK), f32),
            pltpu.VMEM((7, 24, BLK), f32),
            pltpu.VMEM((24, BLK), f32),
            pltpu.SemaphoreType.DMA((total,)),
            pltpu.SemaphoreType.DMA((total,)),
            pltpu.SemaphoreType.DMA((STEPS,)),
            pltpu.SemaphoreType.DMA((4,)),
            pltpu.SemaphoreType.DMA((2, 2)),
            pltpu.SemaphoreType.DMA((2, 2)),
            pltpu.SemaphoreType.DMA((4,)),
        ],
        compiler_params=pltpu.CompilerParams(
            collective_id=0, has_side_effects=True, vmem_limit_bytes=48 << 20),
        name="propagate",
    )(h, p, part)


def extended_2(block, sides, width):
    for axis, dim in sides:
        count = lax.axis_size(axis)
        forward = [(i, i + 1) for i in range(count - 1)]
        backward = [(target, source) for source, target in forward]
        low = lax.ppermute(
            lax.slice_in_dim(block, block.shape[dim] - width, None, axis=dim), axis, forward
        )
        high = lax.ppermute(lax.slice_in_dim(block, 0, width, axis=dim), axis, backward)
        block = jnp.concatenate([low, block, high], axis=dim)
    return block


def partial_integrals(potential, basis):
    width_x, width_y, depth_z = potential.shape
    extended = extended_2(potential, (("row", 0), ("col", 1)), 1)
    padded = jnp.pad(extended, ((0, 0), (0, 0), (1, 1)))
    beside = padded[2:, 1:-1, 1:-1] + padded[:-2, 1:-1, 1:-1]
    beside = beside + padded[1:-1, 2:, 1:-1] + padded[1:-1, :-2, 1:-1]
    beside = beside + padded[1:-1, 1:-1, 2:] + padded[1:-1, 1:-1, :-2]
    effective = potential + KAPPA * (beside - 6.0 * potential)
    blocks_here = basis.shape[2] // BLK
    weighted = (basis * effective[:, :, None, :]).astype(jnp.bfloat16)
    return jnp.einsum(
        "xykaz,xykbz->kab",
        weighted.reshape(width_x, width_y, blocks_here, BLK, depth_z),
        basis.reshape(width_x, width_y, blocks_here, BLK, depth_z),
        preferred_element_type=jnp.float32,
    )


def shards(potential, basis, hamiltonian, density, hmask, pmask):
    part = partial_integrals(potential, basis).reshape(STEPS, 2, ROWS, BLK)
    row_start = lax.axis_index("row") * 3
    col_start = lax.axis_index("col") * 3
    hpattern = lax.dynamic_slice(hmask, (row_start, col_start), (3, 3))
    ppattern = lax.dynamic_slice(pmask, (row_start, col_start), (3, 3))
    masked_h = (
        hamiltonian.reshape(3, BLK, 3, BLK) * hpattern[:, None, :, None].astype(jnp.bfloat16)
    ).reshape(STEPS, 2, ROWS, WIDE)
    masked_p = (
        density.reshape(2, 3, BLK, 3, BLK) * ppattern[None, :, None, :, None].astype(jnp.bfloat16)
    ).reshape(2, WIDE, WIDE)
    units = jnp.stack([
        jnp.concatenate(
            [masked_p[0, :, t * BLK:(t + 1) * BLK], masked_p[1, :, t * BLK:(t + 1) * BLK],
             masked_p[0, :, 256 + 64 * t:320 + 64 * t], masked_p[1, :, 256 + 64 * t:320 + 64 * t]],
            axis=1)
        for t in range(2)
    ]).reshape(2, STEPS, 2, ROWS, WIDE)
    result = propagate(masked_h, units, part).reshape(2, WIDE, WIDE)
    whole = jnp.stack([
        jnp.concatenate(
            [result[0, :, t * BLK:(t + 1) * BLK], result[1, :, t * BLK:(t + 1) * BLK],
             result[0, :, 256 + 64 * t:320 + 64 * t], result[1, :, 256 + 64 * t:320 + 64 * t]],
            axis=1)
        for t in range(2)
    ])
    whole = whole.reshape(2, 3, BLK, 3, BLK) * ppattern[None, :, None, :, None].astype(jnp.bfloat16)
    return whole.reshape(2, WIDE, WIDE)


def solution(mesh):
    in_specs = (
        P("row", "col", None),
        P("row", "col", None, None),
        P("row", "col"),
        P(None, "row", "col"),
        P(),
        P(),
    )
    out_specs = P(None, "row", "col")
    return jax.shard_map(shards, mesh=mesh, in_specs=in_specs, out_specs=out_specs, check_vma=False)
```

time: 730 us -> 157 us (0.22)
  waiting for transfers between devices: 667 us -> 1.68 us
  Pallas kernels: 0 us -> 130 us
  matrix products: 21.9 us -> 0.97 us
  between operations: 13.3 us -> 0.21 us
    all_gather x3 -> x0, waiting for transfers between devices: 489 us -> none  [the longest x2 406 us: apply(): column_whole = lax.all_gather(operand, 'row', axis=1, tiled=True)]
    psum x1 -> x0, waiting for transfers between devices: 175 us -> none  [shards(): summed = lax.psum(partial_blocks, 'col')]
    pallas_call x0 -> x1, Pallas kernels: none -> 130 us  [propagate(): pl.pallas_call(functools.partial(core_kernel, order), out_shape=jax.Shape...]
    dot_general x5 -> x1, matrix products: 21.9 us -> 0.97 us  [partial_integrals(): jnp.einsum('xykaz,xykbz->kab', weighted.reshape(width_x, width_y, blocks_...]
  transfers between devices with their start and end apart: 8 -> 4, of which waited for: 5 -> 2; matrix products, arithmetic and copies ran while one was open for 1% -> 1% of each run, Pallas kernels for 0% -> 0%
where the time goes in v1:
time: 157 us; the launch traced here: 156 us
  Pallas kernels  130 us (83%)
  starting transfers between devices  17.3 us (11%)
  other arithmetic  3.05 us (2%)
  local copies, waits for them, and re-layouts  2.21 us (1%)
  waiting for transfers between devices  1.68 us (1%)
    pallas_call x1, Pallas kernels, propagate(): pl.pallas_call(functools.partial(core_kernel, order), out_shape=jax.Shape...  130 us
    ppermute x2, starting transfers between devices, extended_2(): lax.ppermute(lax.slice_in_dim(block, block.shape[dim] - width, None, axis...  12.2 us
    ppermute x2, starting transfers between devices, extended_2(): lax.ppermute(lax.slice_in_dim(block, 0, width, axis=dim), axis, backward)  5.12 us
  transfers between devices with their start and end apart: 4, of which 2 were waited for; matrix products, arithmetic and copies ran while one was open for 1% of the time, Pallas kernels for 0%

profile of v1, /device:TPU:1, one launch (start us, length us, event | category | flops | bytes accessed | tf_op | source)
XLA Modules:
  0.0 155.6 jit_solution(11409408256396857492)
XLA Ops:
  0.0 0.8 fusion.10
  0.8 4.3 %collective-permute-start.1 = (f32[1,4,512]{2,1,0:T(4,128)S(1)}, f32[1,4,512]{2,1,0:T(4,128)S(1)}, u32[]{:S(2)}, u32[]{:S(2)}) collective-permute-start(f32[1,4,512]{2,1,0:T(4,128)S(1)} %get-tuple-element.24), channel_id=1, source_target_pairs={{0,16},{16,32},{32,48},{48,64},{64,80},{80,96},{96,112},{112,128},... | collective-permute-start | bytes 24584 | tf_op jit(solution)/shard_map/ppermute | solution.py:564
  5.1 1.3 collective-permute-start
  6.4 0.8 dynamic-slice_convert_fusion
  7.2 0.2 mul.65
  7.6 0.1 fusion.7
  7.7 0.1 broadcast_bitcast_fusion
  7.7 0.7 copy-done.2
  8.5 0.1 fusion.8
  8.6 1.1 collective-permute-done
  9.7 3.8 %collective-permute-start.2 = (f32[4,1,512]{2,1,0:T(1,128)S(1)}, f32[4,1,512]{2,1,0:T(1,128)S(1)}, u32[]{:S(2)}, u32[]{:S(2)}) collective-permute-start(f32[4,1,512]{2,1,0:T(1,128)S(1)} %get-tuple-element.22), channel_id=1, source_target_pairs={{1,0},{2,1},{3,2},{4,3},{5,4},{6,5},{7,6},{8,7},{9,8},{10,9},{11,1... | collective-permute-start | bytes 24584 | tf_op jit(solution)/shard_map/ppermute | solution.py:567
  13.6 7.8 %collective-permute-start.3 = (f32[4,1,512]{2,1,0:T(1,128)S(1)}, f32[4,1,512]{2,1,0:T(1,128)S(1)}, u32[]{:S(2)}, u32[]{:S(2)}) collective-permute-start(f32[4,1,512]{2,1,0:T(1,128)S(1)} %get-tuple-element.21), channel_id=1, source_target_pairs={{0,1},{1,2},{2,3},{3,4},{4,5},{5,6},{6,7},{7,8},{8,9},{9,10},{10,1... | collective-permute-start | bytes 24584 | tf_op jit(solution)/shard_map/ppermute | solution.py:564
  21.4 0.1 maximum_maximum_fusion.p_ref
  21.6 0.6 collective-permute-done.3
  22.2 0.1 select_maximum_fusion
  22.3 0.1 fusion.3
  22.4 0.7 multiply_convert_fusion
  23.1 1.0 fusion.11
  24.1 130.2 %propagate.1 = bf16[2,3,2,64,384]{4,3,2,1,0:T(8,128)(2,1)S(1)} custom-call(bf16[3,2,64,384]{3,2,1,0:T(8,128)(2,1)S(1)} %broadcast_multiply_fusion.1.h_ref, bf16[2,3,2,64,384]{4,3,2,1,0:T(8,128)(2,1)S(1)} %maximum_maximum_fusion.p_ref, f32[3,2,64,128]{3,2,1,0:T(8,128)S(1)} %bitcast.51), custom_call_target="tpu_custom_call" | custom-call | tf_op jit(solution)/shard_map/propagate/pallas_call | solution.py:528
  154.3 0.1 slice_bitcast_fusion.5
  154.4 0.1 slice_bitcast_fusion.7
  154.5 0.1 maximum_bitcast_fusion
  154.6 0.1 maximum_bitcast_fusion.1
  154.7 0.9 maximum_multiply_fusion
  (17 shorter events, 0.2 us)
Async XLA Ops:
  0.0 7.5 %copy-start.1 = (bf16[2,384,384]{2,1,0:T(8,128)(2,1)S(1)}, bf16[2,384,384]{2,1,0:T(8,128)(2,1)}, u32[]{:S(2)}) copy-start(bf16[2,384,384]{2,1,0:T(8,128)(2,1)} %param.9) | copy-start | bytes 1769476
  0.8 7.8 %collective-permute-start.1 = (f32[1,4,512]{2,1,0:T(4,128)S(1)}, f32[1,4,512]{2,1,0:T(4,128)S(1)}, u32[]{:S(2)}, u32[]{:S(2)}) collective-permute-start(f32[1,4,512]{2,1,0:T(4,128)S(1)} %get-tuple-element.24), channel_id=1, source_target_pairs={{0,16},{16,32},{32,48},{48,64},{64,80},{80,96},{96,112},{112,128},... | collective-permute-start | bytes 24584 | tf_op jit(solution)/shard_map/ppermute | solution.py:564
  5.1 4.6 %collective-permute-start = (f32[1,4,512]{2,1,0:T(4,128)S(1)}, f32[1,4,512]{2,1,0:T(4,128)S(1)}, u32[]{:S(2)}, u32[]{:S(2)}) collective-permute-start(f32[1,4,512]{2,1,0:T(4,128)S(1)} %get-tuple-element.23), channel_id=1, source_target_pairs={{16,0},{32,16},{48,32},{64,48},{80,64},{96,80},{112,96},{128,112},... | collective-permute-start | bytes 24584 | tf_op jit(solution)/shard_map/ppermute | solution.py:567
  7.5 1.0 copy-start.2
  7.6 1.1 copy-start.3
  8.4 14.0 %copy-start = (bf16[2,4,384,512]{3,2,1,0:T(8,128)(2,1)S(1)}, bf16[2,4,384,512]{3,2,1,0:T(8,128)(2,1)}, u32[]{:S(2)}) copy-start(bf16[2,4,384,512]{3,2,1,0:T(8,128)(2,1)} %param.7) | copy-start | bytes 9437188
  9.7 11.8 %collective-permute-start.2 = (f32[4,1,512]{2,1,0:T(1,128)S(1)}, f32[4,1,512]{2,1,0:T(1,128)S(1)}, u32[]{:S(2)}, u32[]{:S(2)}) collective-permute-start(f32[4,1,512]{2,1,0:T(1,128)S(1)} %get-tuple-element.22), channel_id=1, source_target_pairs={{1,0},{2,1},{3,2},{4,3},{5,4},{6,5},{7,6},{8,7},{9,8},{10,9},{11,1... | collective-permute-start | bytes 24584 | tf_op jit(solution)/shard_map/ppermute | solution.py:567
  13.6 8.6 %collective-permute-start.3 = (f32[4,1,512]{2,1,0:T(1,128)S(1)}, f32[4,1,512]{2,1,0:T(1,128)S(1)}, u32[]{:S(2)}, u32[]{:S(2)}) collective-permute-start(f32[4,1,512]{2,1,0:T(1,128)S(1)} %get-tuple-element.21), channel_id=1, source_target_pairs={{0,1},{1,2},{2,3},{3,4},{4,5},{5,6},{6,7},{7,8},{8,9},{9,10},{10,1... | collective-permute-start | bytes 24584 | tf_op jit(solution)/shard_map/ppermute | solution.py:564

commit v2 on v1

--- a/solution.py
+++ b/solution.py
@@ -14,7 +14,7 @@
 MESH = pl.DeviceIdType.MESH
 
 STEPS = 3
-Y_FIRST = (16, 16, 32)
+Y_FIRST = (32, 16, 16)
 ROWS = 64
 WIDE = 384
 
@@ -67,15 +67,16 @@
         for dx in (0, -1, 1, 2):
             out["Pm", dx, rb] = ("m", 144, [("P", dx, rb)], ("Pm", dx, rb))
     for s in range(STEPS):
-        out["Fx+", s] = ("x+", 192, [("F", 0, s)], ("F", -1, s))
-        out["Fx-", s] = ("x-", 192, [("F", 0, s)], ("F", 1, s))
-        out["F2+", s] = ("x+", 96, [("F", -1, s)], ("F2", 0, s))
-        out["F2-", s] = ("x-", 96, [("F", 1, s)], ("F2", 1, s))
-        for dx in (0, -1, 1):
-            out["Fm", dx, s] = ("m", 192, [("F", dx, s)], ("Fm", dx, s))
         for e in (0, 1):
-            out["Fm2", e, s] = ("m", 96, [("F2", e, s)], ("Fm2", e, s))
-    out["Dm",] = ("m", 96, [], ("Dm",))
+            out["Fx+", s, e] = ("x+", 96, [("F", 0, s)], ("F", -1, s, e))
+            out["Fx-", s, 1 - e] = ("x-", 96, [("F", 0, s)], ("F", 1, s, 1 - e))
+        out["F2+", s] = ("x+", 96, [("F", -1, s, 0)], ("F", 2, s, 0))
+        out["F2-", s] = ("x-", 96, [("F", 1, s, 1)], ("F", 2, s, 1))
+        out["Fm", 0, s] = ("m", 192, [("F", 0, s)], ("Fm", 0, s))
+        for dx in (-1, 1, 2):
+            for e in (0, 1):
+                out["Fm", dx, s, e] = ("m", 96, [("F", dx, s, e)], ("Fm", dx, s, e))
+    out["Dm",] = ("m", 96, [("I", i) for i in range(4)], ("Dm",))
     for j in range(1, 8):
         out["Dr", j] = ("z+" if j % 2 else "y+", 12, [("Dc",)], ("Dr", j))
     for j in range(1, 4):
@@ -97,17 +98,20 @@
         near = [("b", s, dy, dz) for dy in (0, -1, 1) for dz in range(-up, down + 1)]
         near += [("A4", s, dz) for dz in range(-up, down + 1) if dz] + [("a", s, 2)]
         far = [("b", s, 2, dz) for dz in range(-up, down + 1)]
-        out["C1", s] = (3.2, near + far + every_p, [("C1", s)])
-        out["Ff", s] = (0.5, [("C1", s)] + every_d, [("F", 0, s)])
+        out["C1", s, 0] = (2.4, near + every_p, [("C1", s, 0)])
+        out["C1", s, 1] = (0.8, far + [("C1", s, 0)], [("C1", s, 1)])
+        out["Ff", s] = (0.5, [("C1", s, 1)] + every_d, [("F", 0, s)])
+    out["E",] = (0.5, [("halo",)], [("E",)])
+    for i in range(4):
+        out["I", i] = (1.5, [("E",)], [("I", i)])
     out["Dc",] = (0.2, [("Dm",)], [("Dc",)])
     out["Df",] = (0.2, [("Dc",)] + [("Dr", j) for j in range(1, 8)], [("Df",)])
-    all_a = [("C1", s) for s in range(STEPS)]
+    all_a = [("C1", s, 1) for s in range(STEPS)]
     for s in range(STEPS):
         out["S", s, 0] = (0.9, all_a + [("F", 0, s), ("Fm", 0, s)], [("S", s, 0)])
-        out["S", s, -1] = (0.8, all_a + [("F", -1, s), ("Fm", -1, s)], [("S", s, -1)])
-        out["S", s, 1] = (0.8, all_a + [("F", 1, s), ("Fm", 1, s)], [("S", s, 1)])
-        far = [("F2", e, s) for e in (0, 1)] + [("Fm2", e, s) for e in (0, 1)]
-        out["S", s, 2] = (0.8, all_a + far, [("S", s, 2)])
+        for dx in (-1, 1, 2):
+            needs = [(k, dx, s, e) for k in ("F", "Fm") for e in (0, 1)]
+            out["S", s, dx] = (0.8, all_a + needs, [("S", s, dx)])
     return out
 
 
@@ -133,9 +137,10 @@
     arrivals = []
     order = []
     now = 0.0
-    free["z+"] = free["z-"] = 2 * 144 / LINK_RATE / 1.0
+    free["z+"] = free["z-"] = 2 * 144 / LINK_RATE
     for rb in range(4):
-        heapq.heappush(arrivals, (16.0 + rb, 0, ("P0", rb)))
+        heapq.heappush(arrivals, (20.0 + rb, 0, ("P0", rb)))
+    heapq.heappush(arrivals, (4.0, 0, ("halo",)))
     count = 0
 
     def issue():
@@ -151,7 +156,8 @@
             free[link] = end
             sent.add(name)
             count += 1
-            heapq.heappush(arrivals, (end + (1.0 if link == "m" else 1.8), count, name))
+            wait = 6.0 if name[0] in ("Dr", "Dy", "Dz") else 1.0 if link == "m" else 1.8
+            heapq.heappush(arrivals, (end + wait, count, name))
             order.append(("send", name))
 
     while len(done) < len(work) or arrivals:
@@ -159,7 +165,12 @@
         if arrivals and arrivals[0][0] <= now:
             _, _, name = heapq.heappop(arrivals)
             order.append(("wait", name))
-            have.add(("P", 0, name[1]) if name[0] == "P0" else every[name][3])
+            if name[0] == "P0":
+                have.add(("P", 0, name[1]))
+            elif name[0] == "halo":
+                have.add(name)
+            else:
+                have.add(every[name][3])
             continue
         ready = [n for n, w in work.items() if n not in done and all(d in have for d in w[1])]
         if ready:
@@ -176,14 +187,17 @@
     return order, now
 
 
-def core_kernel(order, h_ref, p_ref, part_ref, out_ref, a_buf, b_buf, f_buf, o_buf,
+def core_kernel(order, h_ref, p_ref, pot_ref, basis_ref, out_ref, a_buf, b_buf, f_buf, o_buf,
                 f_acc, s_acc, d_mate, d_chip, d_all, d_got, d_fin,
-                send_sem, recv_sem, local_sem, pin_sem, pin_send, ret_sem, ret_send):
+                basis_buf, halo, eff, part,
+                send_sem, recv_sem, local_sem, pin_sem, pin_send, ret_sem, ret_send,
+                halo_sem, halo_send, basis_sem):
     row, col = lax.axis_index("row"), lax.axis_index("col")
     x, zl = row // 4, row % 4
     y, zh, c = col // 4, (col // 2) % 2, col % 2
     z = zh * 4 + zl
-    half = c
+    basis_copy = pltpu.make_async_copy(basis_ref, basis_buf, basis_sem)
+    basis_copy.start()
 
     def dev(dx=0, dy=0, dz=0, core=None):
         zz = (z + dz) % 8
@@ -198,6 +212,9 @@
     friends += [dev(dy=j) for j in (1, 2, 3)] + [dev(dz=j) for j in range(1, 8)]
     friends += [dev(dy=j, dz=4) for j in (1, 2, 3)]
     friends += [dev_line((zl + j) % 4, 1 - c) for j in (1, 2, 3)]
+    beside = [((row + 1) % 16, col), ((row + 15) % 16, col), (row, (col + 1) % 16),
+              (row, (col + 15) % 16)]
+    friends += beside
     for friend in friends:
         pl.semaphore_signal(barrier, inc=1, device_id=friend, device_id_type=MESH)
     pl.semaphore_wait(barrier, len(friends))
@@ -224,6 +241,7 @@
         return f_buf.at[(x + dx) % 4, rbs, s, core]
 
     FULL, LOW, HIGH = pl.ds(0, 4), pl.ds(0, 2), pl.ds(2, 2)
+    PAIR = (LOW, HIGH)
 
     def ends(name):
         kind = name[0]
@@ -285,11 +303,13 @@
             src = b_slot(dx, rb, c)
             return src, src, b_slot(dx, rb, 1 - c), dev(core=1 - c)
         if kind == "Fx+":
-            src = f_slot(0, name[1], c, FULL)
-            return src, src, f_slot(-1, name[1], c, FULL), dev(dx=1)
+            _, s, e = name
+            src = f_slot(0, s, c, PAIR[e])
+            return src, src, f_slot(-1, s, c, PAIR[e]), dev(dx=1)
         if kind == "Fx-":
-            src = f_slot(0, name[1], c, FULL)
-            return src, src, f_slot(1, name[1], c, FULL), dev(dx=-1)
+            _, s, e = name
+            src = f_slot(0, s, c, PAIR[e])
+            return src, src, f_slot(1, s, c, PAIR[e]), dev(dx=-1)
         if kind == "F2+":
             src = f_slot(-1, name[1], c, LOW)
             return src, src, f_slot(2, name[1], c, LOW), dev(dx=1)
@@ -297,16 +317,12 @@
             src = f_slot(1, name[1], c, HIGH)
             return src, src, f_slot(2, name[1], c, HIGH), dev(dx=-1)
         if kind == "Fm":
-            _, dx, s = name
-            src = f_slot(dx, s, c, FULL)
-            return src, src, f_slot(dx, s, 1 - c, FULL), dev(core=1 - c)
-        if kind == "Fm2":
-            _, e, s = name
-            rbs = HIGH if e else LOW
-            src = f_slot(2, s, c, rbs)
-            return src, src, f_slot(2, s, 1 - c, rbs), dev(core=1 - c)
+            dx, s = name[1:3]
+            rbs = PAIR[name[3]] if len(name) > 3 else FULL
+            src = f_slot(dx, s, c, rbs)
+            return src, src, f_slot(dx, s, 1 - c, rbs), dev(core=1 - c)
         if kind == "Dm":
-            return part_ref.at[:, 1 - c], d_mate, d_mate, dev(core=1 - c)
+            return part.at[:, 1 - c], d_mate, d_mate, dev(core=1 - c)
         if kind == "Dr":
             j = name[1]
             dy, dz = j // 2, 4 * (j % 2)
@@ -336,6 +352,29 @@
             src_ref=land, dst_ref=land, send_sem=send_sem.at[i], recv_sem=recv_sem.at[i],
             device_id=target, device_id_type=MESH)
 
+    to_side = [row < 15, row > 0, col < 15, col > 0]
+    from_side = [row > 0, row < 15, col > 0, col < 15]
+
+    def halo_copy(i):
+        return pltpu.make_async_remote_copy(
+            src_ref=pot_ref, dst_ref=halo.at[i], send_sem=halo_send.at[i],
+            recv_sem=halo_sem.at[i], device_id=beside[i], device_id_type=MESH)
+
+    for i in range(4):
+        @pl.when(to_side[i])
+        def _():
+            halo_copy(i).start()
+
+    def wait_halo():
+        for i in range(4):
+            @pl.when(from_side[i])
+            def _():
+                halo_copy(i).wait_recv()
+
+            @pl.when(jnp.logical_not(from_side[i]))
+            def _():
+                halo[i] = jnp.zeros((2, 4, 512), jnp.float32)
+
     own = [pltpu.make_async_copy(h_ref.at[s, c], a_buf.at[s, y, zh, zl, :, lanes(c)],
                                  local_sem.at[s]) for s in range(STEPS)]
     for copy in own:
@@ -373,16 +412,17 @@
     def chunk_a(s, yy, zz):
         return a_buf[s, yy, zz].reshape(4 * ROWS, 2 * WIDE)
 
-    def first_product(s):
-        f_acc[s] = jnp.zeros((4 * ROWS, WIDE), jnp.float32)
+    def first_product(s, far):
+        if not far:
+            f_acc[s] = jnp.zeros((4 * ROWS, WIDE), jnp.float32)
 
         def body(k, carry):
-            yy, zz = k // 2, k % 2
+            yy, zz = (y + (k // 2) + 3) % 4, k % 2
             right = b_buf[yy, pl.ds(zz * 2, 2)].reshape(2 * WIDE, WIDE)
             f_acc[s] += jnp.dot(chunk_a(s, yy, zz), right, preferred_element_type=jnp.float32)
             return carry
 
-        lax.fori_loop(0, 8, body, 0)
+        lax.fori_loop(6 if far else 0, 8 if far else 6, body, 0)
 
     def diagonal(rb, s):
         return d_all[rb].reshape(STEPS, ROWS, BLK)[s].astype(jnp.bfloat16)
@@ -417,6 +457,42 @@
                 s_acc[s, rows] += jnp.dot(diagonal(rb, s), right,
                                           preferred_element_type=jnp.float32)
 
+    def screen():
+        wait_halo()
+        zero = jnp.zeros((1, 1), jnp.float32)
+        for i in range(2):
+            for j in range(4):
+                here = pot_ref[i, j:j + 1]
+                below = pot_ref[0, j:j + 1] if i else halo[0, 1, j:j + 1]
+                above = halo[1, 0, j:j + 1] if i else pot_ref[1, j:j + 1]
+                left = pot_ref[i, j - 1:j] if j else halo[2, i, 3:4]
+                right = pot_ref[i, j + 1:j + 2] if j < 3 else halo[3, i, 0:1]
+                later = jnp.concatenate([here[:, 1:], zero], axis=1)
+                earlier = jnp.concatenate([zero, here[:, :-1]], axis=1)
+                total = above + below
+                total = total + right + left
+                total = total + later + earlier
+                eff[i, j:j + 1] = here + KAPPA * (total - 6.0 * here)
+
+    def integrate(i):
+        if i == 0:
+            basis_copy.wait()
+            part[...] = jnp.zeros_like(part)
+
+        def body(j, carry):
+            cell = 2 * i + j
+            table = basis_buf[cell // 4, cell % 4]
+            scale = eff[cell // 4, pl.ds(cell % 4, 1)]
+            weighted = (table.astype(jnp.float32) * scale).astype(jnp.bfloat16)
+            for k in range(3):
+                rows = slice(k * BLK, (k + 1) * BLK)
+                more = lax.dot_general(weighted[rows], table[rows], (((1,), (1,)), ((), ())),
+                                       preferred_element_type=jnp.float32)
+                part[k] += more.reshape(2, ROWS, BLK)
+            return carry
+
+        lax.fori_loop(0, 2, body, 0)
+
     def finish_integrals():
         mine = y * 2 + zh
         total = d_chip[mine]
@@ -430,14 +506,18 @@
         kind = name[0]
         if kind == "Hready":
             own[name[1]].wait()
+        elif kind == "E":
+            screen()
+        elif kind == "I":
+            integrate(name[1])
         elif kind == "C1":
-            first_product(name[1])
+            first_product(name[1], name[2])
         elif kind == "Ff":
             first_finish(name[1])
         elif kind == "S":
             second_product(name[1], name[2])
         elif kind == "Dc":
-            d_chip[...] = (part_ref[:, c] + d_mate[...]).reshape(8, 24, BLK)
+            d_chip[...] = (part[:, c] + d_mate[...]).reshape(8, 24, BLK)
         elif kind == "Df":
             finish_integrals()
 
@@ -447,6 +527,8 @@
         if what == "send":
             outgoing(name).start()
         elif what == "wait":
+            if name[0] == "halo":
+                continue
             if name[0] == "P0":
                 rb = name[1]
                 land = b_buf.at[x, rb, :, c]
@@ -517,9 +599,13 @@
         @pl.when(jnp.logical_not(here))
         def _():
             remote().wait_send()
-
-
-def propagate(h, p, part):
+    for i in range(4):
+        @pl.when(to_side[i])
+        def _():
+            halo_copy(i).wait_send()
+
+
+def propagate(h, p, potential, basis):
     order, _ = schedule()
     total = len(messages())
     bf, f32 = jnp.bfloat16, jnp.float32
@@ -528,7 +614,7 @@
     return pl.pallas_call(
         functools.partial(core_kernel, order),
         out_shape=jax.ShapeDtypeStruct((2, STEPS, 2, ROWS, WIDE), bf),
-        in_specs=[any_space, any_space, vmem],
+        in_specs=[any_space, any_space, vmem, any_space],
         out_specs=any_space,
         scratch_shapes=[
             pltpu.VMEM((STEPS, 4, 2, 4, ROWS, 2 * WIDE), bf),
@@ -542,6 +628,10 @@
             pltpu.VMEM((4, 4, 2, 24, BLK), f32),
             pltpu.VMEM((7, 24, BLK), f32),
             pltpu.VMEM((24, BLK), f32),
+            pltpu.VMEM((2, 4, WIDE, 512), bf),
+            pltpu.VMEM((4, 2, 4, 512), f32),
+            pltpu.VMEM((2, 4, 512), f32),
+            pltpu.VMEM((STEPS, 2, ROWS, BLK), f32),
             pltpu.SemaphoreType.DMA((total,)),
             pltpu.SemaphoreType.DMA((total,)),
             pltpu.SemaphoreType.DMA((STEPS,)),
@@ -549,46 +639,17 @@
             pltpu.SemaphoreType.DMA((2, 2)),
             pltpu.SemaphoreType.DMA((2, 2)),
             pltpu.SemaphoreType.DMA((4,)),
+            pltpu.SemaphoreType.DMA((4,)),
+            pltpu.SemaphoreType.DMA((4,)),
+            pltpu.SemaphoreType.DMA,
         ],
         compiler_params=pltpu.CompilerParams(
             collective_id=0, has_side_effects=True, vmem_limit_bytes=48 << 20),
         name="propagate",
-    )(h, p, part)
-
-
-def extended_2(block, sides, width):
-    for axis, dim in sides:
-        count = lax.axis_size(axis)
-        forward = [(i, i + 1) for i in range(count - 1)]
-        backward = [(target, source) for source, target in forward]
-        low = lax.ppermute(
-            lax.slice_in_dim(block, block.shape[dim] - width, None, axis=dim), axis, forward
-        )
-        high = lax.ppermute(lax.slice_in_dim(block, 0, width, axis=dim), axis, backward)
-        block = jnp.concatenate([low, block, high], axis=dim)
-    return block
-
-
-def partial_integrals(potential, basis):
-    width_x, width_y, depth_z = potential.shape
-    extended = extended_2(potential, (("row", 0), ("col", 1)), 1)
-    padded = jnp.pad(extended, ((0, 0), (0, 0), (1, 1)))
-    beside = padded[2:, 1:-1, 1:-1] + padded[:-2, 1:-1, 1:-1]
-    beside = beside + padded[1:-1, 2:, 1:-1] + padded[1:-1, :-2, 1:-1]
-    beside = beside + padded[1:-1, 1:-1, 2:] + padded[1:-1, 1:-1, :-2]
-    effective = potential + KAPPA * (beside - 6.0 * potential)
-    blocks_here = basis.shape[2] // BLK
-    weighted = (basis * effective[:, :, None, :]).astype(jnp.bfloat16)
-    return jnp.einsum(
-        "xykaz,xykbz->kab",
-        weighted.reshape(width_x, width_y, blocks_here, BLK, depth_z),
-        basis.reshape(width_x, width_y, blocks_here, BLK, depth_z),
-        preferred_element_type=jnp.float32,
-    )
+    )(h, p, potential, basis)
 
 
 def shards(potential, basis, hamiltonian, density, hmask, pmask):
-    part = partial_integrals(potential, basis).reshape(STEPS, 2, ROWS, BLK)
     row_start = lax.axis_index("row") * 3
     col_start = lax.axis_index("col") * 3
     hpattern = lax.dynamic_slice(hmask, (row_start, col_start), (3, 3))
@@ -606,7 +667,7 @@
             axis=1)
         for t in range(2)
     ]).reshape(2, STEPS, 2, ROWS, WIDE)
-    result = propagate(masked_h, units, part).reshape(2, WIDE, WIDE)
+    result = propagate(masked_h, units, potential, basis).reshape(2, WIDE, WIDE)
     whole = jnp.stack([
         jnp.concatenate(
             [result[0, :, t * BLK:(t + 1) * BLK], result[1, :, t * BLK:(t + 1) * BLK],

time: 157 us -> 133 us (0.85)
  starting transfers between devices: 17.3 us -> 0 us
  Pallas kernels: 130 us -> 128 us
  waiting for transfers between devices: 1.68 us -> 0 us
    ppermute x4 -> x0, starting transfers between devices: 17.3 us -> none  [the longest x2 12.2 us: extended_2(): lax.ppermute(lax.slice_in_dim(block, block.shape[dim] - width, None, axis...]
    pallas_call x1, Pallas kernels: 130 us -> 128 us  [propagate(): pl.pallas_call(functools.partial(core_kernel, order), out_shape=jax.Shape...]
    ppermute x4 -> x0, waiting for transfers between devices: 1.68 us -> none  [the longest x2 1.07 us: extended_2(): lax.ppermute(lax.slice_in_dim(block, 0, width, axis=dim), axis, backward)]
  transfers between devices with their start and end apart: 4 -> 0, of which waited for: 2 -> 0; matrix products, arithmetic and copies ran while one was open for 1% -> 0% of each run, Pallas kernels for 0% -> 0%
where the time goes in v2:
time: 133 us; the launch traced here: 132 us
  Pallas kernels  128 us (96%)
  other arithmetic  2.21 us (2%)
  local copies, waits for them, and re-layouts  2.13 us (2%)
    pallas_call x1, Pallas kernels, propagate(): pl.pallas_call(functools.partial(core_kernel, order), out_shape=jax.Shape...  128 us

profile of v2, /device:TPU:1, one launch (start us, length us, event | category | flops | bytes accessed | tf_op | source)
XLA Modules:
  0.0 132.1 jit_solution(14320536740304841156)
XLA Ops:
  0.0 0.0 copy-start.2
  0.0 0.9 dynamic-slice_convert_fusion
  0.9 0.2 mul.45
  1.1 0.0 copy-done.2
  1.1 0.0 copy-start.3
  1.1 0.1 broadcast_multiply_fusion
  1.2 0.0 copy-start
  1.2 0.1 fusion
  1.3 0.1 fusion.1
  1.4 0.0 copy-start.1
  1.4 0.1 maximum_maximum_fusion.p_ref
  1.6 0.1 broadcast_bitcast_fusion
  1.6 0.4 copy-done.3
  2.1 1.0 copy-done
  3.1 0.0 copy-done.1
  3.1 127.6 %propagate.1 = bf16[2,3,2,64,384]{4,3,2,1,0:T(8,128)(2,1)S(1)} custom-call(bf16[3,2,64,384]{3,2,1,0:T(8,128)(2,1)S(1)} %broadcast_multiply_fusion.1.h_ref, bf16[2,3,2,64,384]{4,3,2,1,0:T(8,128)(2,1)S(1)} %maximum_maximum_fusion.p_ref, f32[2,4,512]{2,1,0:T(4,128)S(1)} %copy-done.1, bf16[2,4,384,512]{3,2,1,0:T(8,128)(2,1)S(1)} %copy-done), custom_call_target="tpu_custom_call" | custom-call | tf_op jit(solution)/shard_map/propagate/pallas_call | solution.py:614
  130.7 0.1 slice_bitcast_fusion.5
  130.9 0.1 slice_bitcast_fusion.7
  130.9 0.1 maximum_bitcast_fusion
  131.0 0.1 maximum_bitcast_fusion.1
  131.2 0.9 maximum_multiply_fusion
  (3 shorter events, 0.1 us)
Async XLA Ops:
  0.0 1.1 copy-start.2
  1.1 1.0 copy-start.3
  1.2 1.9 %copy-start = (bf16[2,4,384,512]{3,2,1,0:T(8,128)(2,1)S(1)}, bf16[2,4,384,512]{3,2,1,0:T(8,128)(2,1)}, u32[]{:S(2)}) copy-start(bf16[2,4,384,512]{3,2,1,0:T(8,128)(2,1)} %basis_ref.1) | copy-start | bytes 9437188
  1.4 1.7 %copy-start.1 = (f32[2,4,512]{2,1,0:T(4,128)S(1)}, f32[2,4,512]{2,1,0:T(4,128)}, u32[]{:S(2)}) copy-start(f32[2,4,512]{2,1,0:T(4,128)} %pot_ref.1) | copy-start | bytes 49156

commit v3 on v2

--- a/solution.py
+++ b/solution.py
@@ -14,8 +14,8 @@
 MESH = pl.DeviceIdType.MESH
 
 STEPS = 3
-Y_FIRST = (32, 16, 16)
 ROWS = 64
+CHUNKS = ((0, 0, 64, 16), (1, 0, 64, 32), (2, 0, 32, 16), (2, 32, 32, 0))
 WIDE = 384
 
 
@@ -30,8 +30,9 @@
 def messages():
     out = {}
     for s in range(STEPS):
-        a_kb, b_kb = Y_FIRST[s] * 1.5, (ROWS - Y_FIRST[s]) * 1.5
         out["Hm", s] = ("m", 48, [], ("H", s))
+    for s, (_, _, rows, y_first) in enumerate(CHUNKS):
+        a_kb, b_kb = y_first * 1.5, (rows - y_first) * 1.5
         up, down = plus_hops(s), 7 - plus_hops(s)
         for t in range(1, up + 1):
             out["bz+", s, t] = ("z+", b_kb, [("b", s, 0, 1 - t)], ("b", s, 0, -t))
@@ -44,6 +45,8 @@
                 out["by2", s, dz] = ("y+", b_kb, [("b", s, -1, dz)], ("b", s, 2, dz))
             else:
                 out["by2", s, dz] = ("y-", b_kb, [("b", s, 1, dz)], ("b", s, 2, dz))
+        if not y_first:
+            continue
         out["ay+", s] = ("y+", a_kb, [("a", s, 0)], ("a", s, -1))
         out["ay-", s] = ("y-", a_kb, [("a", s, 0)], ("a", s, 1))
         if s % 2 == 0:
@@ -66,58 +69,71 @@
             out["Px2", rb] = ("x-", 144, [("P", 1, rb)], ("P", 2, rb))
         for dx in (0, -1, 1, 2):
             out["Pm", dx, rb] = ("m", 144, [("P", dx, rb)], ("Pm", dx, rb))
-    for s in range(STEPS):
+    for s, (_, _, rows, _) in enumerate(CHUNKS):
+        kb = rows * 1.5
         for e in (0, 1):
-            out["Fx+", s, e] = ("x+", 96, [("F", 0, s)], ("F", -1, s, e))
-            out["Fx-", s, 1 - e] = ("x-", 96, [("F", 0, s)], ("F", 1, s, 1 - e))
-        out["F2+", s] = ("x+", 96, [("F", -1, s, 0)], ("F", 2, s, 0))
-        out["F2-", s] = ("x-", 96, [("F", 1, s, 1)], ("F", 2, s, 1))
-        out["Fm", 0, s] = ("m", 192, [("F", 0, s)], ("Fm", 0, s))
+            out["Fx+", s, e] = ("x+", kb, [("F", 0, s)], ("F", -1, s, e))
+            out["Fx-", s, 1 - e] = ("x-", kb, [("F", 0, s)], ("F", 1, s, 1 - e))
+        out["F2+", s] = ("x+", kb, [("F", -1, s, 0)], ("F", 2, s, 0))
+        out["F2-", s] = ("x-", kb, [("F", 1, s, 1)], ("F", 2, s, 1))
+        out["Fm", 0, s] = ("m", 2 * kb, [("F", 0, s)], ("Fm", 0, s))
         for dx in (-1, 1, 2):
             for e in (0, 1):
-                out["Fm", dx, s, e] = ("m", 96, [("F", dx, s, e)], ("Fm", dx, s, e))
+                out["Fm", dx, s, e] = ("m", kb, [("F", dx, s, e)], ("Fm", dx, s, e))
     out["Dm",] = ("m", 96, [("I", i) for i in range(4)], ("Dm",))
-    for j in range(1, 8):
-        out["Dr", j] = ("z+" if j % 2 else "y+", 12, [("Dc",)], ("Dr", j))
     for j in range(1, 4):
-        out["Dy", j] = ("y-", 12, [("Df",)], ("Dy", j))
-    for j in range(1, 8):
-        out["Dz", j] = ("z-", 48, [("Df",)] + [("Dy", i) for i in (1, 2, 3)], ("Dz", j))
+        out["Dr", j] = ("y-" if j == 3 else "y+", 12 if j != 2 else 24, [("Dc",)], ("Dr", j))
+    for k in (1, -1, 2, -2, 3, -3, 4):
+        out["Dz", k] = ("z+" if k > 0 else "z-", 12 * abs(k), [("Dl",)], ("Dz", k))
+    for j in range(1, 4):
+        out["Dy", j] = ("y-" if j == 3 else "y+", 48 if j != 2 else 96, [("Df",)], ("Dy", j))
     return out
 
 
 def tasks():
     out = {}
     for s in range(STEPS):
-        out["Hready", s] = (0.05, [("H", s)], [("b", s, 0, 0), ("a", s, 0)])
+        gives = [(k, i, 0, 0) if k == "b" else (k, i, 0)
+                 for i, chunk in enumerate(CHUNKS) if chunk[0] == s for k in "ba"]
+        out["Hready", s] = (0.05, [("H", s)], gives)
     every_p = [("P", dx, rb) for dx in (0, -1, 1, 2) for rb in range(4)]
     every_p += [("Pm", dx, rb) for dx in (0, -1, 1, 2) for rb in range(4)]
-    every_d = [("Dy", i) for i in (1, 2, 3)] + [("Dz", i) for i in range(1, 8)] + [("Df",)]
-    for s in range(STEPS):
+    every_d = [("Dy", i) for i in (1, 2, 3)] + [("Df",)]
+    for s, (_, _, rows, y_first) in enumerate(CHUNKS):
         up, down = plus_hops(s), 7 - plus_hops(s)
         near = [("b", s, dy, dz) for dy in (0, -1, 1) for dz in range(-up, down + 1)]
-        near += [("A4", s, dz) for dz in range(-up, down + 1) if dz] + [("a", s, 2)]
+        if y_first:
+            near += [("A4", s, dz) for dz in range(-up, down + 1) if dz] + [("a", s, 2)]
         far = [("b", s, 2, dz) for dz in range(-up, down + 1)]
-        out["C1", s, 0] = (2.4, near + every_p, [("C1", s, 0)])
-        out["C1", s, 1] = (0.8, far + [("C1", s, 0)], [("C1", s, 1)])
+        out["C1", s, 0] = (0.2 + 0.035 * rows, near + every_p, [("C1", s, 0)])
+        out["C1", s, 1] = (0.1 + 0.011 * rows, far + [("C1", s, 0)], [("C1", s, 1)])
         out["Ff", s] = (0.5, [("C1", s, 1)] + every_d, [("F", 0, s)])
     out["E",] = (0.5, [("halo",)], [("E",)])
     for i in range(4):
         out["I", i] = (1.5, [("E",)], [("I", i)])
     out["Dc",] = (0.2, [("Dm",)], [("Dc",)])
-    out["Df",] = (0.2, [("Dc",)] + [("Dr", j) for j in range(1, 8)], [("Df",)])
-    all_a = [("C1", s, 1) for s in range(STEPS)]
-    for s in range(STEPS):
-        out["S", s, 0] = (0.9, all_a + [("F", 0, s), ("Fm", 0, s)], [("S", s, 0)])
+    out["Dl",] = (0.2, [("Dc",)] + [("Dr", j) for j in (1, 2, 3)], [("Dl",)])
+    out["Df",] = (0.2, [("Dl",)] + [("Dz", k) for k in (1, -1, 2, -2, 3, -3, 4)], [("Df",)])
+    all_a = [("C1", s, 1) for s in range(len(CHUNKS))]
+    for t in range(STEPS):
+        mine = [s for s, chunk in enumerate(CHUNKS) if chunk[0] == t]
+        needs = {0: [(k, 0, s) for k in ("F", "Fm") for s in mine]}
         for dx in (-1, 1, 2):
-            needs = [(k, dx, s, e) for k in ("F", "Fm") for e in (0, 1)]
-            out["S", s, dx] = (0.8, all_a + needs, [("S", s, dx)])
+            needs[dx] = [(k, dx, s, e) for k in ("F", "Fm") for e in (0, 1) for s in mine]
+        if t < STEPS - 1:
+            early = [("C1", 0, 1), ("C1", 1, 1)] + sum(needs.values(), [])
+            out["S", t, 9, 0, 2] = (2.2, early, [("S", t, 0)])
+            out["S", t, 9, 2, 3] = (1.1, early + all_a, [("S", t, 1)])
+            continue
+        for dx in (0, -1, 1, 2):
+            out["S", t, dx, 0, 3] = (0.8, all_a + needs[dx], [("S", t, dx)])
     return out
 
 
 RATE = {"m": 200.0}
 LINK_RATE = 42.0
 BACKLOG = 4.0
+D_WAIT = {"Dr": 5.0, "Dz": 6.0, "Dy": 5.0}
 
 
 def rank_of(name):
@@ -150,13 +166,13 @@
         for name in ready:
             link, size, _, _ = every[name]
             start = max(now, free.get(link, 0.0))
-            if start - now > BACKLOG and link != "m":
+            if start - now > BACKLOG and link != "m" and name[0][0] != "D":
                 continue
             end = start + size / RATE.get(link, LINK_RATE)
             free[link] = end
             sent.add(name)
             count += 1
-            wait = 6.0 if name[0] in ("Dr", "Dy", "Dz") else 1.0 if link == "m" else 1.8
+            wait = D_WAIT.get(name[0], 1.0 if link == "m" else 1.8)
             heapq.heappush(arrivals, (end + wait, count, name))
             order.append(("send", name))
 
@@ -188,7 +204,7 @@
 
 
 def core_kernel(order, h_ref, p_ref, pot_ref, basis_ref, out_ref, a_buf, b_buf, f_buf, o_buf,
-                f_acc, s_acc, d_mate, d_chip, d_all, d_got, d_fin,
+                f_acc, s_acc, d_mate, d_chip, d_all, d_got, d_line,
                 basis_buf, halo, eff, part,
                 send_sem, recv_sem, local_sem, pin_sem, pin_send, ret_sem, ret_send,
                 halo_sem, halo_send, basis_sem):
@@ -224,12 +240,14 @@
 
     def block(s, dy, dz, color):
         zz = (z + dz) % 8
-        rows = pl.ds(0, Y_FIRST[s]) if color == "a" else pl.ds(Y_FIRST[s], ROWS - Y_FIRST[s])
-        return a_buf.at[s, (y + dy) % 4, zz // 4, zz % 4, rows]
+        tile, first, count, y_first = CHUNKS[s]
+        rows = pl.ds(first, y_first) if color == "a" else pl.ds(first + y_first, count - y_first)
+        return a_buf.at[tile, (y + dy) % 4, zz // 4, zz % 4, rows]
 
     def block4(s, dz):
         zz = (z + dz) % 8
-        return a_buf.at[s, :, zz // 4, zz % 4, pl.ds(0, Y_FIRST[s])]
+        tile, first, _, y_first = CHUNKS[s]
+        return a_buf.at[tile, :, zz // 4, zz % 4, pl.ds(first, y_first)]
 
     def lanes(core):
         return pl.ds(pl.multiple_of(core * WIDE, 128), WIDE)
@@ -238,7 +256,8 @@
         return b_buf.at[(x + dx) % 4, rb, :, core]
 
     def f_slot(dx, s, core, rbs):
-        return f_buf.at[(x + dx) % 4, rbs, s, core]
+        tile, first, count, _ = CHUNKS[s]
+        return f_buf.at[(x + dx) % 4, rbs, tile, core, pl.ds(first, count)]
 
     FULL, LOW, HIGH = pl.ds(0, 4), pl.ds(0, 2), pl.ds(2, 2)
     PAIR = (LOW, HIGH)
@@ -325,17 +344,16 @@
             return part.at[:, 1 - c], d_mate, d_mate, dev(core=1 - c)
         if kind == "Dr":
             j = name[1]
-            dy, dz = j // 2, 4 * (j % 2)
-            to = ((y + dy) % 4) * 2 + (zh + j % 2) % 2
-            return d_chip.at[to], d_got.at[j - 1], d_got.at[j - 1], dev(dy=dy, dz=dz)
+            return d_chip.at[(y + j) % 4], d_got.at[j - 1], d_got.at[j - 1], dev(dy=j)
+        if kind == "Dz":
+            k = name[1]
+            zz = (z - k) % 8
+            src = d_line.at[zh, zl]
+            return src, src, d_line.at[zz // 4, zz % 4], dev(dz=k)
         if kind == "Dy":
             j = name[1]
-            return d_fin, d_all.at[zl, y, zh], d_all.at[zl, (y - j) % 4, zh], dev(dy=j)
-        if kind == "Dz":
-            j = name[1]
-            zz = (z - j) % 8
-            src = d_all.at[zl, :, zh]
-            return src, src, d_all.at[zz % 4, :, zz // 4], dev(dz=j)
+            src = d_all.at[:, y]
+            return src, src, d_all.at[:, (y - j) % 4], dev(dy=j)
         raise KeyError(name)
 
     def outgoing(name):
@@ -409,53 +427,54 @@
                 def _():
                     remote().start()
 
-    def chunk_a(s, yy, zz):
-        return a_buf[s, yy, zz].reshape(4 * ROWS, 2 * WIDE)
-
     def first_product(s, far):
+        tile, first, count, _ = CHUNKS[s]
+        rows = slice(first, first + count)
         if not far:
-            f_acc[s] = jnp.zeros((4 * ROWS, WIDE), jnp.float32)
+            f_acc[tile, :, rows] = jnp.zeros((4, count, WIDE), jnp.float32)
 
         def body(k, carry):
             yy, zz = (y + (k // 2) + 3) % 4, k % 2
+            left = a_buf[tile, yy, zz, :, rows].reshape(4 * count, 2 * WIDE)
             right = b_buf[yy, pl.ds(zz * 2, 2)].reshape(2 * WIDE, WIDE)
-            f_acc[s] += jnp.dot(chunk_a(s, yy, zz), right, preferred_element_type=jnp.float32)
+            more = jnp.dot(left, right, preferred_element_type=jnp.float32)
+            f_acc[tile, :, rows] += more.reshape(4, count, WIDE)
             return carry
 
         lax.fori_loop(6 if far else 0, 8 if far else 6, body, 0)
 
     def diagonal(rb, s):
-        return d_all[rb].reshape(STEPS, ROWS, BLK)[s].astype(jnp.bfloat16)
+        return d_all[rb].astype(jnp.float32).reshape(STEPS, ROWS, BLK)[s].astype(jnp.bfloat16)
 
     def first_finish(s):
+        tile, first, count, _ = CHUNKS[s]
+        rows = slice(first, first + count)
         for rb in range(4):
-            rows = pl.ds(rb * ROWS, ROWS)
-            right = b_buf[x, rb, s].reshape(BLK, WIDE)
-            total = f_acc[s, rows] + jnp.dot(diagonal(rb, s), right,
-                                             preferred_element_type=jnp.float32)
-            f_acc[s, rows] = total
-            f_buf[x, rb, s, c] = total.astype(jnp.bfloat16)
-
-    def second_product(s, dx):
-        xx = (x + dx) % 4
-        tile = slice(s * BLK, (s + 1) * BLK), slice(WIDE + s * BLK, WIDE + (s + 1) * BLK)
+            right = b_buf[x, rb, tile].reshape(BLK, WIDE)
+            total = f_acc[tile, rb, rows] + jnp.dot(diagonal(rb, tile)[rows], right,
+                                                    preferred_element_type=jnp.float32)
+            f_acc[tile, rb, rows] = total
+            f_buf[x, rb, tile, c, rows] = total.astype(jnp.bfloat16)
+
+    def second_product(s, dx, low, high):
+        cuts = [slice(e * WIDE + s * BLK, e * WIDE + (s + 1) * BLK) for e in range(2)]
 
         def body(k, carry):
-            t, zz = k // 2, k % 2
+            xx, t = (x + (k // (high - low) if dx == 9 else dx)) % 4, low + k % (high - low)
             left = jnp.concatenate(
-                [a_buf[t, xx, zz, :, :, cut].reshape(4 * ROWS, BLK) for cut in tile], axis=1)
-            right = jnp.concatenate(
-                [f_buf[xx, zz * 2 + e, s].reshape(BLK, WIDE) for e in range(2)], axis=0)
-            s_acc[t] += jnp.dot(left, right, preferred_element_type=jnp.float32)
+                [a_buf[t, xx, zz, :, :, cut].reshape(4 * ROWS, BLK)
+                 for zz in range(2) for cut in cuts], axis=1)
+            right = f_buf[xx, :, s].reshape(4 * BLK, WIDE)
+            more = jnp.dot(left, right, preferred_element_type=jnp.float32)
+            s_acc[t] += more.reshape(4, ROWS, WIDE)
             return carry
 
-        lax.fori_loop(0, 6, body, 0)
-        if dx == 0:
+        lax.fori_loop(0, (4 if dx == 9 else 1) * (high - low), body, 0)
+        if dx in (0, 9) and low <= s < high:
             for rb in range(4):
-                rows = pl.ds(rb * ROWS, ROWS)
                 right = f_buf[x, rb, s].reshape(BLK, WIDE)
-                s_acc[s, rows] += jnp.dot(diagonal(rb, s), right,
-                                          preferred_element_type=jnp.float32)
+                s_acc[s, rb] += jnp.dot(diagonal(rb, s), right,
+                                        preferred_element_type=jnp.float32)
 
     def screen():
         wait_halo()
@@ -493,14 +512,16 @@
 
         lax.fori_loop(0, 2, body, 0)
 
+    def line_integrals():
+        total = d_chip[y].astype(jnp.float32)
+        for j in range(3):
+            total = total + d_got[j].astype(jnp.float32)
+        d_line[zh, zl] = total.astype(jnp.bfloat16)
+
     def finish_integrals():
-        mine = y * 2 + zh
-        total = d_chip[mine]
-        for j in range(7):
-            total = total + d_got[j]
         factor = float(BLK * 2 * 64 * 512) ** -0.5
-        d_fin[...] = total * factor
-        d_all[zl, y, zh] = total * factor
+        total = d_line[0].astype(jnp.float32) + d_line[1].astype(jnp.float32)
+        d_all[:, y] = (total * factor).astype(jnp.bfloat16)
 
     def run(name):
         kind = name[0]
@@ -515,9 +536,11 @@
         elif kind == "Ff":
             first_finish(name[1])
         elif kind == "S":
-            second_product(name[1], name[2])
+            second_product(*name[1:])
         elif kind == "Dc":
-            d_chip[...] = (part[:, c] + d_mate[...]).reshape(8, 24, BLK)
+            d_chip[...] = (part[:, c] + d_mate[...]).reshape(4, 48, BLK).astype(jnp.bfloat16)
+        elif kind == "Dl":
+            line_integrals()
         elif kind == "Df":
             finish_integrals()
 
@@ -558,16 +581,15 @@
         return here, local, remote
 
     for rb in range(4):
-        rows = pl.ds(rb * ROWS, ROWS)
         for s in range(STEPS):
             base = b_buf[x, rb, s, c].astype(jnp.float32)
-            f = f_acc[s, rows]
+            f = f_acc[s, rb]
             mixed = f[:, 2 * BLK:]
             turned = pltpu.roll(mixed, BLK // 2, 1)
             turn = jnp.concatenate(
                 [f[:, BLK:2 * BLK], -f[:, :BLK], jnp.where(lane < BLK // 2, turned, -turned)],
                 axis=1)
-            o_buf[rb, s] = (base + TIME_STEP * turn - quarter * s_acc[s, rows]).astype(jnp.bfloat16)
+            o_buf[rb, s] = (base + TIME_STEP * turn - quarter * s_acc[s, rb]).astype(jnp.bfloat16)
         here, local, remote = back(rb)
 
         @pl.when(here)
@@ -621,13 +643,13 @@
             pltpu.VMEM((4, 4, STEPS, 2, ROWS, WIDE), bf),
             pltpu.VMEM((4, 4, STEPS, 2, ROWS, WIDE), bf),
             pltpu.VMEM((4, STEPS, ROWS, WIDE), bf),
-            pltpu.VMEM((STEPS, 4 * ROWS, WIDE), f32),
-            pltpu.VMEM((STEPS, 4 * ROWS, WIDE), f32),
+            pltpu.VMEM((STEPS, 4, ROWS, WIDE), f32),
+            pltpu.VMEM((STEPS, 4, ROWS, WIDE), f32),
             pltpu.VMEM((STEPS, ROWS, BLK), f32),
-            pltpu.VMEM((8, 24, BLK), f32),
-            pltpu.VMEM((4, 4, 2, 24, BLK), f32),
-            pltpu.VMEM((7, 24, BLK), f32),
-            pltpu.VMEM((24, BLK), f32),
+            pltpu.VMEM((4, 48, BLK), bf),
+            pltpu.VMEM((4, 4, 48, BLK), bf),
+            pltpu.VMEM((3, 48, BLK), bf),
+            pltpu.VMEM((2, 4, 48, BLK), bf),
             pltpu.VMEM((2, 4, WIDE, 512), bf),
             pltpu.VMEM((4, 2, 4, 512), f32),
             pltpu.VMEM((2, 4, 512), f32),
@@ -644,7 +666,7 @@
             pltpu.SemaphoreType.DMA,
         ],
         compiler_params=pltpu.CompilerParams(
-            collective_id=0, has_side_effects=True, vmem_limit_bytes=48 << 20),
+            collective_id=0, has_side_effects=True, vmem_limit_bytes=60 << 20),
         name="propagate",
     )(h, p, potential, basis)
 

time: 133 us -> 123 us (0.925)
  Pallas kernels: 128 us -> 115 us
  other arithmetic: 2.21 us -> 3.73 us
    pallas_call x1, Pallas kernels: 128 us -> 115 us  [propagate(): pl.pallas_call(functools.partial(core_kernel, order), out_shape=jax.Shape...]
    unnamed x11 -> x7, local copies, waits for them, and re-layouts: 1.57 us -> 0.14 us
where the time goes in v3:
time: 123 us; the launch traced here: 121 us
  Pallas kernels  115 us (93%)
  other arithmetic  3.73 us (3%)
  local copies, waits for them, and re-layouts  2.73 us (2%)
    pallas_call x1, Pallas kernels, propagate(): pl.pallas_call(functools.partial(core_kernel, order), out_shape=jax.Shape...  115 us

profile of v3, /device:TPU:1, one launch (start us, length us, event | category | flops | bytes accessed | tf_op | source)
XLA Modules:
  0.0 121.5 jit_solution(18084331662396079111)
XLA Ops:
  0.0 0.0 copy-start
  0.0 0.9 dynamic-slice_convert_fusion
  0.9 0.2 mul.45
  1.1 0.0 copy-done
  1.1 0.1 broadcast_multiply_fusion
  1.2 0.1 fusion
  1.2 0.0 copy-start.1
  1.3 0.1 fusion.1
  1.4 1.0 maximum_maximum_fusion.p_ref
  2.4 0.1 broadcast_bitcast_fusion
  2.4 0.0 copy-done.1
  2.4 0.7 broadcast_multiply_fusion.1.h_ref
  3.2 114.9 %propagate.1 = bf16[2,3,2,64,384]{4,3,2,1,0:T(8,128)(2,1)} custom-call(bf16[3,2,64,384]{3,2,1,0:T(8,128)(2,1)} %broadcast_multiply_fusion.1.h_ref, bf16[2,3,2,64,384]{4,3,2,1,0:T(8,128)(2,1)} %maximum_maximum_fusion.p_ref, f32[2,4,512]{2,1,0:T(4,128)} %pot_ref.1, bf16[2,4,384,512]{3,2,1,0:T(8,128)(2,1)} %basis_ref.1), custom_call_target="tpu_custom_call" | custom-call | tf_op jit(solution)/shard_map/propagate/pallas_call | solution.py:636
  118.1 1.2 slice_bitcast_fusion.5
  119.3 1.1 slice_bitcast_fusion.7
  120.3 0.1 maximum_bitcast_fusion
  120.4 0.1 maximum_bitcast_fusion.1
  120.6 0.9 maximum_multiply_fusion
  (2 shorter events, 0.1 us)
Async XLA Ops:
  0.0 1.1 copy-start
  1.2 1.2 copy-start.1

commit v4 on v3

--- a/solution.py
+++ b/solution.py
@@ -17,6 +17,13 @@
 ROWS = 64
 CHUNKS = ((0, 0, 64, 16), (1, 0, 64, 32), (2, 0, 32, 16), (2, 32, 32, 0))
 WIDE = 384
+
+
+LANES = ((0, 2 * BLK), (2 * BLK, BLK), (0, WIDE))
+
+
+def groups(s):
+    return (1, 0) if s == len(CHUNKS) - 1 else (2,)
 
 
 def plus_hops(s):
@@ -70,16 +77,18 @@
         for dx in (0, -1, 1, 2):
             out["Pm", dx, rb] = ("m", 144, [("P", dx, rb)], ("Pm", dx, rb))
     for s, (_, _, rows, _) in enumerate(CHUNKS):
-        kb = rows * 1.5
-        for e in (0, 1):
-            out["Fx+", s, e] = ("x+", kb, [("F", 0, s)], ("F", -1, s, e))
-            out["Fx-", s, 1 - e] = ("x-", kb, [("F", 0, s)], ("F", 1, s, 1 - e))
-        out["F2+", s] = ("x+", kb, [("F", -1, s, 0)], ("F", 2, s, 0))
-        out["F2-", s] = ("x-", kb, [("F", 1, s, 1)], ("F", 2, s, 1))
-        out["Fm", 0, s] = ("m", 2 * kb, [("F", 0, s)], ("Fm", 0, s))
-        for dx in (-1, 1, 2):
+        for g in groups(s):
+            kb = rows * 1.5 * LANES[g][1] / WIDE
             for e in (0, 1):
-                out["Fm", dx, s, e] = ("m", kb, [("F", dx, s, e)], ("Fm", dx, s, e))
+                out["Fx+", s, e, g] = ("x+", kb, [("F", 0, s)], ("F", -1, s, e, g))
+                out["Fx-", s, 1 - e, g] = ("x-", kb, [("F", 0, s)], ("F", 1, s, 1 - e, g))
+            out["F2+", s, 0, g] = ("x+", kb, [("F", -1, s, 0, g)], ("F", 2, s, 0, g))
+            out["F2-", s, 1, g] = ("x-", kb, [("F", 1, s, 1, g)], ("F", 2, s, 1, g))
+            out["Fm", 0, s, 2, g] = ("m", 2 * kb, [("F", 0, s)], ("Fm", 0, s, g))
+            for dx in (-1, 1, 2):
+                for e in (0, 1):
+                    out["Fm", dx, s, e, g] = ("m", kb, [("F", dx, s, e, g)],
+                                              ("Fm", dx, s, e, g))
     out["Dm",] = ("m", 96, [("I", i) for i in range(4)], ("Dm",))
     for j in range(1, 4):
         out["Dr", j] = ("y-" if j == 3 else "y+", 12 if j != 2 else 24, [("Dc",)], ("Dr", j))
@@ -115,18 +124,28 @@
     out["Dl",] = (0.2, [("Dc",)] + [("Dr", j) for j in (1, 2, 3)], [("Dl",)])
     out["Df",] = (0.2, [("Dl",)] + [("Dz", k) for k in (1, -1, 2, -2, 3, -3, 4)], [("Df",)])
     all_a = [("C1", s, 1) for s in range(len(CHUNKS))]
-    for t in range(STEPS):
-        mine = [s for s, chunk in enumerate(CHUNKS) if chunk[0] == t]
-        needs = {0: [(k, 0, s) for k in ("F", "Fm") for s in mine]}
-        for dx in (-1, 1, 2):
-            needs[dx] = [(k, dx, s, e) for k in ("F", "Fm") for e in (0, 1) for s in mine]
-        if t < STEPS - 1:
-            early = [("C1", 0, 1), ("C1", 1, 1)] + sum(needs.values(), [])
-            out["S", t, 9, 0, 2] = (2.2, early, [("S", t, 0)])
-            out["S", t, 9, 2, 3] = (1.1, early + all_a, [("S", t, 1)])
-            continue
+    def first_of(t, dx, g):
+        got = []
+        for s, chunk in enumerate(CHUNKS):
+            if chunk[0] == t:
+                for h in groups(s) if g == 2 else (g,) if g in groups(s) else (2,):
+                    if dx == 0:
+                        got += [("F", 0, s), ("Fm", 0, s, h)]
+                    else:
+                        got += [(k, dx, s, e, h) for k in ("F", "Fm") for e in (0, 1)]
+        return got
+
+    for t in range(STEPS - 1):
+        early = [("C1", 0, 1), ("C1", 1, 1)]
+        early += sum([first_of(t, dx, 2) for dx in (0, -1, 1, 2)], [])
+        out["S", t, 9, 0, 2, 2] = (2.2, early, [("S", t, 0)])
+        out["S", t, 9, 2, 3, 2] = (1.1, early + all_a, [("S", t, 1)])
+    gone = [("S", t, i) for t in range(STEPS - 1) for i in (0, 1)]
+    t = STEPS - 1
+    for g in (1, 0):
         for dx in (0, -1, 1, 2):
-            out["S", t, dx, 0, 3] = (0.8, all_a + needs[dx], [("S", t, dx)])
+            out["S", t, dx, 0, 3, g] = (0.5, all_a + first_of(t, dx, g), [("S", t, dx, g)])
+        out["R", g] = (0.6, gone + [("S", t, dx, g) for dx in (0, -1, 1, 2)], [("R", g)])
     return out
 
 
@@ -203,9 +222,9 @@
     return order, now
 
 
-def core_kernel(order, h_ref, p_ref, pot_ref, basis_ref, out_ref, a_buf, b_buf, f_buf, o_buf,
+def core_kernel(order, ham_ref, den_ref, pot_ref, basis_ref, hmask_ref, pmask_ref, out_ref, a_buf, b_buf, f_buf, o_buf,
                 f_acc, s_acc, d_mate, d_chip, d_all, d_got, d_line,
-                basis_buf, halo, eff, part,
+                basis_buf, halo, eff, part, h_ref, p_ref,
                 send_sem, recv_sem, local_sem, pin_sem, pin_send, ret_sem, ret_send,
                 halo_sem, halo_send, basis_sem):
     row, col = lax.axis_index("row"), lax.axis_index("col")
@@ -233,6 +252,12 @@
     friends += beside
     for friend in friends:
         pl.semaphore_signal(barrier, inc=1, device_id=friend, device_id_type=MESH)
+    for t in range(3):
+        for j in range(3):
+            keep = hmask_ref[row * 3 + t, col * 3 + j].astype(jnp.float32)
+            tile = ham_ref[t * BLK:(t + 1) * BLK, j * BLK:(j + 1) * BLK].astype(jnp.float32) * keep
+            h_ref[t, :, :, j * BLK:(j + 1) * BLK] = (
+                tile.astype(jnp.bfloat16).reshape(2, ROWS, BLK))
     pl.semaphore_wait(barrier, len(friends))
 
     names = list(messages())
@@ -255,12 +280,12 @@
     def b_slot(dx, rb, core):
         return b_buf.at[(x + dx) % 4, rb, :, core]
 
-    def f_slot(dx, s, core, rbs):
+    def f_slot(dx, s, core, rbs, g):
         tile, first, count, _ = CHUNKS[s]
-        return f_buf.at[(x + dx) % 4, rbs, tile, core, pl.ds(first, count)]
+        return f_buf.at[(x + dx) % 4, rbs, tile, core, pl.ds(first, count), pl.ds(*LANES[g])]
 
     FULL, LOW, HIGH = pl.ds(0, 4), pl.ds(0, 2), pl.ds(2, 2)
-    PAIR = (LOW, HIGH)
+    PAIR = (LOW, HIGH, FULL)
 
     def ends(name):
         kind = name[0]
@@ -321,25 +346,16 @@
             _, dx, rb = name
             src = b_slot(dx, rb, c)
             return src, src, b_slot(dx, rb, 1 - c), dev(core=1 - c)
-        if kind == "Fx+":
-            _, s, e = name
-            src = f_slot(0, s, c, PAIR[e])
-            return src, src, f_slot(-1, s, c, PAIR[e]), dev(dx=1)
-        if kind == "Fx-":
-            _, s, e = name
-            src = f_slot(0, s, c, PAIR[e])
-            return src, src, f_slot(1, s, c, PAIR[e]), dev(dx=-1)
-        if kind == "F2+":
-            src = f_slot(-1, name[1], c, LOW)
-            return src, src, f_slot(2, name[1], c, LOW), dev(dx=1)
-        if kind == "F2-":
-            src = f_slot(1, name[1], c, HIGH)
-            return src, src, f_slot(2, name[1], c, HIGH), dev(dx=-1)
+        if kind in ("Fx+", "Fx-", "F2+", "F2-"):
+            _, s, e, g = name
+            way = 1 if kind[2] == "+" else -1
+            frm, to = (0, -way) if kind[1] == "x" else (-way, 2)
+            src = f_slot(frm, s, c, PAIR[e], g)
+            return src, src, f_slot(to, s, c, PAIR[e], g), dev(dx=way)
         if kind == "Fm":
-            dx, s = name[1:3]
-            rbs = PAIR[name[3]] if len(name) > 3 else FULL
-            src = f_slot(dx, s, c, rbs)
-            return src, src, f_slot(dx, s, 1 - c, rbs), dev(core=1 - c)
+            _, dx, s, e, g = name
+            src = f_slot(dx, s, c, PAIR[e], g)
+            return src, src, f_slot(dx, s, 1 - c, PAIR[e], g), dev(core=1 - c)
         if kind == "Dm":
             return part.at[:, 1 - c], d_mate, d_mate, dev(core=1 - c)
         if kind == "Dr":
@@ -414,6 +430,27 @@
 
         return here, local, remote
 
+    def pack_p():
+        lane = lax.broadcasted_iota(jnp.int32, (BLK, BLK), 1)
+
+        def put(hf, t, j, value):
+            p_ref[hf, t, :, :, j * BLK:(j + 1) * BLK] = (
+                value.astype(jnp.bfloat16).reshape(2, ROWS, BLK))
+
+        for t in range(3):
+            tiles = []
+            for j in range(3):
+                keep = pmask_ref[row * 3 + t, col * 3 + j].astype(jnp.float32)
+                tiles.append([
+                    den_ref[p, t * BLK:(t + 1) * BLK, j * BLK:(j + 1) * BLK].astype(jnp.float32)
+                    * keep for p in range(2)])
+            for j in range(2):
+                for p in range(2):
+                    put(j, t, p, tiles[j][p])
+            turned = [pltpu.roll(v, BLK // 2, 1) for v in tiles[2]]
+            put(0, t, 2, jnp.where(lane < BLK // 2, tiles[2][0], turned[1]))
+            put(1, t, 2, jnp.where(lane < BLK // 2, turned[0], tiles[2][1]))
+
     def start_p():
         for hf in range(2):
             for r in range(2):
@@ -456,7 +493,8 @@
             f_acc[tile, rb, rows] = total
             f_buf[x, rb, tile, c, rows] = total.astype(jnp.bfloat16)
 
-    def second_product(s, dx, low, high):
+    def second_product(s, dx, low, high, g):
+        lane = slice(LANES[g][0], sum(LANES[g]))
         cuts = [slice(e * WIDE + s * BLK, e * WIDE + (s + 1) * BLK) for e in range(2)]
 
         def body(k, carry):
@@ -464,17 +502,17 @@
             left = jnp.concatenate(
                 [a_buf[t, xx, zz, :, :, cut].reshape(4 * ROWS, BLK)
                  for zz in range(2) for cut in cuts], axis=1)
-            right = f_buf[xx, :, s].reshape(4 * BLK, WIDE)
+            right = f_buf[xx, :, s, :, :, lane].reshape(4 * BLK, LANES[g][1])
             more = jnp.dot(left, right, preferred_element_type=jnp.float32)
-            s_acc[t] += more.reshape(4, ROWS, WIDE)
+            s_acc[t, :, :, lane] += more.reshape(4, ROWS, LANES[g][1])
             return carry
 
         lax.fori_loop(0, (4 if dx == 9 else 1) * (high - low), body, 0)
         if dx in (0, 9) and low <= s < high:
             for rb in range(4):
-                right = f_buf[x, rb, s].reshape(BLK, WIDE)
-                s_acc[s, rb] += jnp.dot(diagonal(rb, s), right,
-                                        preferred_element_type=jnp.float32)
+                right = f_buf[x, rb, s, :, :, lane].reshape(BLK, LANES[g][1])
+                s_acc[s, rb, :, lane] += jnp.dot(diagonal(rb, s), right,
+                                                 preferred_element_type=jnp.float32)
 
     def screen():
         wait_halo()
@@ -523,6 +561,54 @@
         total = d_line[0].astype(jnp.float32) + d_line[1].astype(jnp.float32)
         d_all[:, y] = (total * factor).astype(jnp.bfloat16)
 
+    lane_of = lax.broadcasted_iota(jnp.int32, (ROWS, BLK), 1)
+    quarter = 0.5 * TIME_STEP * TIME_STEP
+    targets = [(zl // 2) * 2 + 1 - zl % 2, 3 - zl, (zl + 2) % 4, zl]
+
+    def back(k, g):
+        lane = pl.ds(*LANES[g])
+        src = o_buf.at[k, :, :, lane]
+        dst = out_ref.at[zl % 2, :, c, :, lane]
+
+        def local():
+            return pltpu.make_async_copy(src, dst, ret_sem.at[zl % 2, c, g])
+
+        def remote():
+            return pltpu.make_async_remote_copy(
+                src_ref=src, dst_ref=dst, send_sem=ret_send.at[k, g],
+                recv_sem=ret_sem.at[zl % 2, c, g],
+                device_id=dev_line(targets[k], zl // 2), device_id_type=MESH)
+
+        return zl // 2 == c, local, remote
+
+    def give_back(g):
+        for k in (1, 2, 0, 3):
+            rb = targets[k]
+            for s in range(STEPS):
+                f = f_acc[s, rb]
+                if g:
+                    turned = pltpu.roll(f[:, 2 * BLK:], BLK // 2, 1)
+                    turn = jnp.where(lane_of < BLK // 2, turned, -turned)
+                else:
+                    turn = jnp.concatenate([f[:, BLK:2 * BLK], -f[:, :BLK]], axis=1)
+                cut = slice(LANES[g][0], sum(LANES[g]))
+                base = b_buf[x, rb, s, c, :, cut].astype(jnp.float32)
+                o_buf[k, s, :, cut] = (
+                    base + TIME_STEP * turn - quarter * s_acc[s, rb, :, cut]
+                ).astype(jnp.bfloat16)
+            here, local, remote = back(k, g)
+            if k < 3:
+                remote().start()
+                continue
+
+            @pl.when(here)
+            def _():
+                local().start()
+
+            @pl.when(jnp.logical_not(here))
+            def _():
+                remote().start()
+
     def run(name):
         kind = name[0]
         if kind == "Hready":
@@ -537,6 +623,8 @@
             first_finish(name[1])
         elif kind == "S":
             second_product(*name[1:])
+        elif kind == "R":
+            give_back(name[1])
         elif kind == "Dc":
             d_chip[...] = (part[:, c] + d_mate[...]).reshape(4, 48, BLK).astype(jnp.bfloat16)
         elif kind == "Dl":
@@ -544,9 +632,13 @@
         elif kind == "Df":
             finish_integrals()
 
-    start_p()
-    s_acc[...] = jnp.zeros_like(s_acc)
+    opened = False
     for what, name in order:
+        if what != "send" and not opened:
+            opened = True
+            pack_p()
+            start_p()
+            s_acc[...] = jnp.zeros_like(s_acc)
         if what == "send":
             outgoing(name).start()
         elif what == "wait":
@@ -561,49 +653,11 @@
         else:
             run(name)
 
-    lane = lax.broadcasted_iota(jnp.int32, (ROWS, BLK), 1)
-    quarter = 0.5 * TIME_STEP * TIME_STEP
-
-    def back(rb):
-        here = (rb == zl) & (zl // 2 == c)
-        src = o_buf.at[rb]
-        dst = out_ref.at[zl % 2, :, c]
-
-        def local():
-            return pltpu.make_async_copy(src, dst, ret_sem.at[zl % 2, c])
-
-        def remote():
-            return pltpu.make_async_remote_copy(
-                src_ref=src, dst_ref=dst, send_sem=ret_send.at[rb],
-                recv_sem=ret_sem.at[zl % 2, c],
-                device_id=dev_line(rb, zl // 2), device_id_type=MESH)
-
-        return here, local, remote
-
-    for rb in range(4):
-        for s in range(STEPS):
-            base = b_buf[x, rb, s, c].astype(jnp.float32)
-            f = f_acc[s, rb]
-            mixed = f[:, 2 * BLK:]
-            turned = pltpu.roll(mixed, BLK // 2, 1)
-            turn = jnp.concatenate(
-                [f[:, BLK:2 * BLK], -f[:, :BLK], jnp.where(lane < BLK // 2, turned, -turned)],
-                axis=1)
-            o_buf[rb, s] = (base + TIME_STEP * turn - quarter * s_acc[s, rb]).astype(jnp.bfloat16)
-        here, local, remote = back(rb)
-
-        @pl.when(here)
-        def _():
-            local().start()
-
-        @pl.when(jnp.logical_not(here))
-        def _():
-            remote().start()
-
-    for hf in range(2):
-        for r in range(2):
-            land = out_ref.at[hf, :, r]
-            pltpu.make_async_copy(land, land, ret_sem.at[hf, r]).wait()
+    for g in range(2):
+        for hf in range(2):
+            for r in range(2):
+                land = out_ref.at[hf, :, r, :, pl.ds(*LANES[g])]
+                pltpu.make_async_copy(land, land, ret_sem.at[hf, r, g]).wait()
 
     for what, name in order:
         if what == "send":
@@ -615,8 +669,10 @@
             @pl.when(jnp.logical_not(here))
             def _():
                 remote().wait_send()
-    for rb in range(4):
-        here, _, remote = back(rb)
+    for g in range(2):
+        for k in range(3):
+            back(k, g)[2]().wait_send()
+        here, _, remote = back(3, g)
 
         @pl.when(jnp.logical_not(here))
         def _():
@@ -627,16 +683,17 @@
             halo_copy(i).wait_send()
 
 
-def propagate(h, p, potential, basis):
+def propagate(h, p, potential, basis, hmask, pmask):
     order, _ = schedule()
     total = len(messages())
     bf, f32 = jnp.bfloat16, jnp.float32
     any_space = pl.BlockSpec(memory_space=pl.ANY)
     vmem = pl.BlockSpec(memory_space=pltpu.VMEM)
+    smem = pl.BlockSpec(memory_space=pltpu.SMEM)
     return pl.pallas_call(
         functools.partial(core_kernel, order),
         out_shape=jax.ShapeDtypeStruct((2, STEPS, 2, ROWS, WIDE), bf),
-        in_specs=[any_space, any_space, vmem, any_space],
+        in_specs=[vmem, vmem, vmem, any_space, smem, smem],
         out_specs=any_space,
         scratch_shapes=[
             pltpu.VMEM((STEPS, 4, 2, 4, ROWS, 2 * WIDE), bf),
@@ -654,13 +711,15 @@
             pltpu.VMEM((4, 2, 4, 512), f32),
             pltpu.VMEM((2, 4, 512), f32),
             pltpu.VMEM((STEPS, 2, ROWS, BLK), f32),
+            pltpu.VMEM((STEPS, 2, ROWS, WIDE), bf),
+            pltpu.VMEM((2, STEPS, 2, ROWS, WIDE), bf),
             pltpu.SemaphoreType.DMA((total,)),
             pltpu.SemaphoreType.DMA((total,)),
             pltpu.SemaphoreType.DMA((STEPS,)),
             pltpu.SemaphoreType.DMA((4,)),
             pltpu.SemaphoreType.DMA((2, 2)),
-            pltpu.SemaphoreType.DMA((2, 2)),
-            pltpu.SemaphoreType.DMA((4,)),
+            pltpu.SemaphoreType.DMA((2, 2, 2)),
+            pltpu.SemaphoreType.DMA((4, 2)),
             pltpu.SemaphoreType.DMA((4,)),
             pltpu.SemaphoreType.DMA((4,)),
             pltpu.SemaphoreType.DMA,
@@ -668,28 +727,14 @@
         compiler_params=pltpu.CompilerParams(
             collective_id=0, has_side_effects=True, vmem_limit_bytes=60 << 20),
         name="propagate",
-    )(h, p, potential, basis)
+    )(h, p, potential, basis, hmask, pmask)
 
 
 def shards(potential, basis, hamiltonian, density, hmask, pmask):
     row_start = lax.axis_index("row") * 3
     col_start = lax.axis_index("col") * 3
-    hpattern = lax.dynamic_slice(hmask, (row_start, col_start), (3, 3))
     ppattern = lax.dynamic_slice(pmask, (row_start, col_start), (3, 3))
-    masked_h = (
-        hamiltonian.reshape(3, BLK, 3, BLK) * hpattern[:, None, :, None].astype(jnp.bfloat16)
-    ).reshape(STEPS, 2, ROWS, WIDE)
-    masked_p = (
-        density.reshape(2, 3, BLK, 3, BLK) * ppattern[None, :, None, :, None].astype(jnp.bfloat16)
-    ).reshape(2, WIDE, WIDE)
-    units = jnp.stack([
-        jnp.concatenate(
-            [masked_p[0, :, t * BLK:(t + 1) * BLK], masked_p[1, :, t * BLK:(t + 1) * BLK],
-             masked_p[0, :, 256 + 64 * t:320 + 64 * t], masked_p[1, :, 256 + 64 * t:320 + 64 * t]],
-            axis=1)
-        for t in range(2)
-    ]).reshape(2, STEPS, 2, ROWS, WIDE)
-    result = propagate(masked_h, units, potential, basis).reshape(2, WIDE, WIDE)
+    result = propagate(hamiltonian, density, potential, basis, hmask, pmask).reshape(2, WIDE, WIDE)
     whole = jnp.stack([
         jnp.concatenate(
             [result[0, :, t * BLK:(t + 1) * BLK], result[1, :, t * BLK:(t + 1) * BLK],

time: 123 us -> 123 us (level)
  Pallas kernels: 115 us -> 118 us
  other arithmetic: 3.73 us -> 1.82 us
    pallas_call x1, Pallas kernels: 115 us -> 118 us  [propagate(): pl.pallas_call(functools.partial(core_kernel, order), out_shape=jax.Shape...]
where the time goes in v4:
time: 123 us
  Pallas kernels  118 us (96%)
  local copies, waits for them, and re-layouts  2.44 us (2%)
  other arithmetic  1.82 us (1%)
    pallas_call x1, Pallas kernels, propagate(): pl.pallas_call(functools.partial(core_kernel, order), out_shape=jax.Shape...  118 us

profile of v4, /device:TPU:1, one launch (start us, length us, event | category | flops | bytes accessed | tf_op | source)
XLA Modules:
  0.0 122.5 jit_solution(14054999102380904477)
XLA Ops:
  0.0 118.2 %propagate.1 = bf16[2,3,2,64,384]{4,3,2,1,0:T(8,128)(2,1)} custom-call(bf16[384,384]{1,0:T(8,128)(2,1)} %ham_ref.1, bf16[2,384,384]{2,1,0:T(8,128)(2,1)} %den_ref.1, f32[2,4,512]{2,1,0:T(4,128)} %pot_ref.1, bf16[2,4,384,512]{3,2,1,0:T(8,128)(2,1)} %basis_ref.1, s32[48,48]{1,0:T(8,128)} %hmask_ref.1, s32[48,48]{1,0:T(8,128)} %pmask_ref.1), custom_call_target="tpu_custom_call" | custom-call | tf_op jit(solution)/shard_map/propagate/pallas_call | solution.py:693
  118.2 1.2 slice_bitcast_fusion.5
  119.4 1.1 slice_bitcast_fusion.7
  120.4 0.1 maximum_bitcast_fusion
  120.6 0.8 dynamic-slice_convert_fusion
  121.4 0.2 mul.21
  121.6 0.9 maximum_multiply_fusion
  (1 shorter events, 0.0 us)

commit v5 on v4

--- a/solution.py
+++ b/solution.py
@@ -222,17 +222,22 @@
     return order, now
 
 
-def core_kernel(order, ham_ref, den_ref, pot_ref, basis_ref, hmask_ref, pmask_ref, out_ref, a_buf, b_buf, f_buf, o_buf,
+def core_kernel(order, ham_in, den_in, pot_in, basis_ref, hmask_ref, pmask_ref, out_ref, a_buf, b_buf, f_buf, o_buf,
                 f_acc, s_acc, d_mate, d_chip, d_all, d_got, d_line,
                 basis_buf, halo, eff, part, h_ref, p_ref,
+                ham_ref, den_ref, pot_ref, third,
                 send_sem, recv_sem, local_sem, pin_sem, pin_send, ret_sem, ret_send,
-                halo_sem, halo_send, basis_sem):
+                halo_sem, halo_send, basis_sem, in_sem, third_sem):
     row, col = lax.axis_index("row"), lax.axis_index("col")
     x, zl = row // 4, row % 4
     y, zh, c = col // 4, (col // 2) % 2, col % 2
     z = zh * 4 + zl
+    ham_copy = pltpu.make_async_copy(ham_in, ham_ref, in_sem.at[0])
+    pot_copy = pltpu.make_async_copy(pot_in, pot_ref, in_sem.at[1])
+    den_copy = pltpu.make_async_copy(den_in, den_ref, in_sem.at[2])
     basis_copy = pltpu.make_async_copy(basis_ref, basis_buf, basis_sem)
-    basis_copy.start()
+    for copy in (ham_copy, pot_copy, den_copy, basis_copy):
+        copy.start()
 
     def dev(dx=0, dy=0, dz=0, core=None):
         zz = (z + dz) % 8
@@ -252,6 +257,7 @@
     friends += beside
     for friend in friends:
         pl.semaphore_signal(barrier, inc=1, device_id=friend, device_id_type=MESH)
+    ham_copy.wait()
     for t in range(3):
         for j in range(3):
             keep = hmask_ref[row * 3 + t, col * 3 + j].astype(jnp.float32)
@@ -394,6 +400,7 @@
             src_ref=pot_ref, dst_ref=halo.at[i], send_sem=halo_send.at[i],
             recv_sem=halo_sem.at[i], device_id=beside[i], device_id_type=MESH)
 
+    pot_copy.wait()
     for i in range(4):
         @pl.when(to_side[i])
         def _():
@@ -431,6 +438,7 @@
         return here, local, remote
 
     def pack_p():
+        den_copy.wait()
         lane = lax.broadcasted_iota(jnp.int32, (BLK, BLK), 1)
 
         def put(hf, t, j, value):
@@ -565,26 +573,51 @@
     quarter = 0.5 * TIME_STEP * TIME_STEP
     targets = [(zl // 2) * 2 + 1 - zl % 2, 3 - zl, (zl + 2) % 4, zl]
 
-    def back(k, g):
-        lane = pl.ds(*LANES[g])
-        src = o_buf.at[k, :, :, lane]
-        dst = out_ref.at[zl % 2, :, c, :, lane]
+    home = y * 4 + zh * 2 + zl // 2
+
+    def landing(hf, r, j):
+        if j == 2:
+            return third.at[hf, :, r]
+        return out_ref.at[j, :, r, :, pl.ds(pl.multiple_of(hf * BLK, BLK), BLK)]
+
+    def back(k, j):
+        src = o_buf.at[k, :, :, pl.ds(j * BLK, BLK)]
+        dst = landing(zl % 2, c, j)
 
         def local():
-            return pltpu.make_async_copy(src, dst, ret_sem.at[zl % 2, c, g])
+            return pltpu.make_async_copy(src, dst, ret_sem.at[zl % 2, c, j])
 
         def remote():
             return pltpu.make_async_remote_copy(
-                src_ref=src, dst_ref=dst, send_sem=ret_send.at[k, g],
-                recv_sem=ret_sem.at[zl % 2, c, g],
+                src_ref=src, dst_ref=dst, send_sem=ret_send.at[k, j],
+                recv_sem=ret_sem.at[zl % 2, c, j],
                 device_id=dev_line(targets[k], zl // 2), device_id_type=MESH)
 
         return zl // 2 == c, local, remote
+
+    def get_back(j):
+        for hf in range(2):
+            for r in range(2):
+                land = landing(hf, r, j)
+                pltpu.make_async_copy(land, land, ret_sem.at[hf, r, j]).wait()
+
+    def unpack_third():
+        lane = lax.broadcasted_iota(jnp.int32, (STEPS * 2 * ROWS, BLK), 1)
+        both = [third[hf].astype(jnp.float32).reshape(STEPS * 2 * ROWS, BLK) for hf in range(2)]
+        turned = [pltpu.roll(v, BLK // 2, 1) for v in both]
+        shape = (STEPS, 2, ROWS, BLK)
+        third[0] = jnp.where(lane < BLK // 2, both[0], turned[1]).astype(jnp.bfloat16).reshape(shape)
+        third[1] = jnp.where(lane < BLK // 2, turned[0], both[1]).astype(jnp.bfloat16).reshape(shape)
+
+    def third_copy(p):
+        return pltpu.make_async_copy(
+            third.at[p], out_ref.at[p, :, :, :, pl.ds(2 * BLK, BLK)], third_sem.at[p])
 
     def give_back(g):
         for k in (1, 2, 0, 3):
             rb = targets[k]
             for s in range(STEPS):
+                keep = pmask_ref[(x * 4 + rb) * 3 + s, home * 3 + (2 if g else zl % 2)]
                 f = f_acc[s, rb]
                 if g:
                     turned = pltpu.roll(f[:, 2 * BLK:], BLK // 2, 1)
@@ -594,20 +627,21 @@
                 cut = slice(LANES[g][0], sum(LANES[g]))
                 base = b_buf[x, rb, s, c, :, cut].astype(jnp.float32)
                 o_buf[k, s, :, cut] = (
-                    base + TIME_STEP * turn - quarter * s_acc[s, rb, :, cut]
-                ).astype(jnp.bfloat16)
-            here, local, remote = back(k, g)
-            if k < 3:
-                remote().start()
-                continue
-
-            @pl.when(here)
-            def _():
-                local().start()
-
-            @pl.when(jnp.logical_not(here))
-            def _():
-                remote().start()
+                    (base + TIME_STEP * turn - quarter * s_acc[s, rb, :, cut])
+                    * keep.astype(jnp.float32)).astype(jnp.bfloat16)
+            for j in (2,) if g else (0, 1):
+                here, local, remote = back(k, j)
+                if k < 3:
+                    remote().start()
+                    continue
+
+                @pl.when(here)
+                def _():
+                    local().start()
+
+                @pl.when(jnp.logical_not(here))
+                def _():
+                    remote().start()
 
     def run(name):
         kind = name[0]
@@ -653,12 +687,10 @@
         else:
             run(name)
 
-    for g in range(2):
-        for hf in range(2):
-            for r in range(2):
-                land = out_ref.at[hf, :, r, :, pl.ds(*LANES[g])]
-                pltpu.make_async_copy(land, land, ret_sem.at[hf, r, g]).wait()
-
+    get_back(2)
+    unpack_third()
+    for p in range(2):
+        third_copy(p).start()
     for what, name in order:
         if what == "send":
             outgoing(name).wait_send()
@@ -669,7 +701,11 @@
             @pl.when(jnp.logical_not(here))
             def _():
                 remote().wait_send()
-    for g in range(2):
+    get_back(0)
+    get_back(1)
+    for p in range(2):
+        third_copy(p).wait()
+    for g in range(3):
         for k in range(3):
             back(k, g)[2]().wait_send()
         here, _, remote = back(3, g)
@@ -688,12 +724,11 @@
     total = len(messages())
     bf, f32 = jnp.bfloat16, jnp.float32
     any_space = pl.BlockSpec(memory_space=pl.ANY)
-    vmem = pl.BlockSpec(memory_space=pltpu.VMEM)
     smem = pl.BlockSpec(memory_space=pltpu.SMEM)
     return pl.pallas_call(
         functools.partial(core_kernel, order),
         out_shape=jax.ShapeDtypeStruct((2, STEPS, 2, ROWS, WIDE), bf),
-        in_specs=[vmem, vmem, vmem, any_space, smem, smem],
+        in_specs=[any_space, any_space, any_space, any_space, smem, smem],
         out_specs=any_space,
         scratch_shapes=[
             pltpu.VMEM((STEPS, 4, 2, 4, ROWS, 2 * WIDE), bf),
@@ -713,16 +748,22 @@
             pltpu.VMEM((STEPS, 2, ROWS, BLK), f32),
             pltpu.VMEM((STEPS, 2, ROWS, WIDE), bf),
             pltpu.VMEM((2, STEPS, 2, ROWS, WIDE), bf),
+            pltpu.VMEM((WIDE, WIDE), bf),
+            pltpu.VMEM((2, WIDE, WIDE), bf),
+            pltpu.VMEM((2, 4, 512), f32),
+            pltpu.VMEM((2, STEPS, 2, ROWS, BLK), bf),
             pltpu.SemaphoreType.DMA((total,)),
             pltpu.SemaphoreType.DMA((total,)),
             pltpu.SemaphoreType.DMA((STEPS,)),
             pltpu.SemaphoreType.DMA((4,)),
             pltpu.SemaphoreType.DMA((2, 2)),
-            pltpu.SemaphoreType.DMA((2, 2, 2)),
-            pltpu.SemaphoreType.DMA((4, 2)),
+            pltpu.SemaphoreType.DMA((2, 2, 3)),
+            pltpu.SemaphoreType.DMA((4, 3)),
             pltpu.SemaphoreType.DMA((4,)),
             pltpu.SemaphoreType.DMA((4,)),
             pltpu.SemaphoreType.DMA,
+            pltpu.SemaphoreType.DMA((3,)),
+            pltpu.SemaphoreType.DMA((2,)),
         ],
         compiler_params=pltpu.CompilerParams(
             collective_id=0, has_side_effects=True, vmem_limit_bytes=60 << 20),
@@ -731,19 +772,8 @@
 
 
 def shards(potential, basis, hamiltonian, density, hmask, pmask):
-    row_start = lax.axis_index("row") * 3
-    col_start = lax.axis_index("col") * 3
-    ppattern = lax.dynamic_slice(pmask, (row_start, col_start), (3, 3))
-    result = propagate(hamiltonian, density, potential, basis, hmask, pmask).reshape(2, WIDE, WIDE)
-    whole = jnp.stack([
-        jnp.concatenate(
-            [result[0, :, t * BLK:(t + 1) * BLK], result[1, :, t * BLK:(t + 1) * BLK],
-             result[0, :, 256 + 64 * t:320 + 64 * t], result[1, :, 256 + 64 * t:320 + 64 * t]],
-            axis=1)
-        for t in range(2)
-    ])
-    whole = whole.reshape(2, 3, BLK, 3, BLK) * ppattern[None, :, None, :, None].astype(jnp.bfloat16)
-    return whole.reshape(2, WIDE, WIDE)
+    result = propagate(hamiltonian, density, potential, basis, hmask, pmask)
+    return result.reshape(2, WIDE, WIDE)
 
 
 def solution(mesh):

time: 123 us -> 120 us (0.976)
  other arithmetic: 1.82 us -> 0 us
    squeeze x2 -> x0, local copies, waits for them, and re-layouts: 2.22 us -> none  [the longest x1 1.16 us: shards(): result[0, :, 256 + 64 * t:320 + 64 * t]]
    unnamed x1, local copies, waits for them, and re-layouts: 0.05 us -> 1.94 us
where the time goes in v5:
time: 120 us
  Pallas kernels  118 us (98%)
  local copies, waits for them, and re-layouts  1.94 us (2%)
    pallas_call x1, Pallas kernels, propagate(): pl.pallas_call(functools.partial(core_kernel, order), out_shape=jax.Shape...  118 us

profile of v5, /device:TPU:1, one launch (start us, length us, event | category | flops | bytes accessed | tf_op | source)
XLA Modules:
  0.0 119.7 jit_solution(2041614119787079997)
XLA Ops:
  0.0 117.8 %propagate.1 = bf16[2,3,2,64,384]{4,3,2,1,0:T(8,128)(2,1)} custom-call(bf16[384,384]{1,0:T(8,128)(2,1)} %ham_in.1, bf16[2,384,384]{2,1,0:T(8,128)(2,1)} %den_in.1, f32[2,4,512]{2,1,0:T(4,128)} %pot_in.1, bf16[2,4,384,512]{3,2,1,0:T(8,128)(2,1)} %basis_ref.1, s32[48,48]{1,0:T(8,128)} %hmask_ref.1, s32[48,48]{1,0:T(8,128)} %pmask_ref.1), custom_call_target="tpu_custom_call" | custom-call | tf_op jit(solution)/shard_map/propagate/pallas_call | solution.py:728
  117.8 1.9 %copy.8 = bf16[2,384,384]{2,1,0:T(8,128)(2,1)} copy(bf16[2,384,384]{2,1,0:T(8,128)(2,1)} %bitcast.1) | data formatting | bytes 1179648
